TPU v7x, 32 devices: a whole 2x2x4 slice. The times are simulated.
32 devices in a mesh: ctx: 8 (over y, x, core), page: 4 (over z).
Axes of the slice: x: 2, y: 2, z: 4, core: 2. Of those that a mesh axis runs over, the one named last changes fastest.
Arguments:
- queries: bfloat16 [2048, 8192], P('ctx', 'page'), may hold values from -200 to 200
- keys: bfloat16 [2048, 512], P('ctx', 'page'), may hold values from -6 to 6
- values: bfloat16 [2048, 512], P('ctx', 'page'), may hold values from -6 to 6
- span_table: int32 [16], replicated, may hold values from 0 to 15, each once
- page_slots: int32 [16], replicated, may hold values from 0 to 15, each once
Outputs:
- attended: bfloat16 [2048, 8192], P('ctx', 'page')
- cache_pages: bfloat16 [16, 4, 2, 128, 128], P('ctx')
- cache_scales: float32 [16, 4, 2], P('ctx')
Inputs may be any that keep to these rules, and one draw needn't show every extreme that they name: Stored span i (rows i * 128 to (i + 1) * 128 - 1) holds prompt positions span_table[i] * 128 onward; every value appears once. `page_slots`: every slot is named by exactly one page.
All inputs are finite; a program needn't handle non-finite values. Where the computation divides by a largest or mean magnitude, that divisor is 1e-20 or more.
Results may differ from a plain program's by a relative error of at most 0.0055.
Values may be sent and summed in bfloat16 or wider, within the bound.
A program may use at most 64 MiB of HBM per device.

v0:
```python
import functools
import math

import jax
import jax.numpy as jnp
from jax import lax
from jax.experimental import pallas as pl
from jax.experimental.pallas import tpu as pltpu
from jax.sharding import PartitionSpec as P

DH = 128
PAGE = 128
SPAN = 128
HIDE = -1e30
MESH = pl.DeviceIdType.MESH


def kernel(
    n, n_page, heads, table_in, slots_in, q_in, k_ref, v_ref,
    out_ref, cache_ref, scales_ref,
    table_ref, slots_ref, q_ref,
    kbuf, vbuf, kmask, vone, acc, top, send, recv, own_sem, page_send, page_recv,
):
    chips = n // 2
    spans = k_ref.shape[0]
    wide = 2 * spans * SPAN
    per = math.gcd(heads, 4)
    groups = heads // per
    size = per * SPAN
    me = lax.axis_index("ctx")
    page = lax.axis_index("page")
    chip = me // 2
    core = me % 2
    sibling = 2 * chip + 1 - core
    rate = DH ** (-0.5) * math.log2(math.e)

    def ahead(d):
        return 2 * ((chip + d) % chips) + core

    def behind(d, c):
        return 2 * ((chip + chips - d) % chips) + c

    local = []

    def fetch(src, dst, j):
        copy = pltpu.make_async_copy(src, dst, own_sem.at[j])
        copy.start()
        local.append(copy)

    barrier = pltpu.get_barrier_semaphore()
    for d in range(1, chips):
        pl.semaphore_signal(barrier, inc=1, device_id={"ctx": ahead(d)}, device_id_type=MESH)
    pl.semaphore_signal(barrier, inc=1, device_id={"ctx": sibling}, device_id_type=MESH)
    for d in range(1, n_page):
        pl.semaphore_signal(
            barrier, inc=1, device_id={"page": (page + d) % n_page}, device_id_type=MESH
        )

    def slot(buf, owner):
        return buf.at[pl.ds(owner * spans, spans)]

    fetch(k_ref, slot(kbuf, me), 0)
    fetch(v_ref, slot(vbuf, me), 1)
    fetch(table_in, table_ref, 2)
    fetch(slots_in, slots_ref, 3)
    fetch(q_in, q_ref, 4)
    pl.semaphore_wait(barrier, chips + n_page - 1)

    def remote(src, buf, owner, index, j, target):
        return pltpu.make_async_remote_copy(
            src_ref=src,
            dst_ref=slot(buf, owner),
            send_sem=send.at[index, j],
            recv_sem=recv.at[index, j],
            device_id={"ctx": target},
            device_id_type=MESH,
        )

    pairs = ((k_ref, kbuf), (v_ref, vbuf))
    started = []
    for d in range(1, chips):
        for j, (src, buf) in enumerate(pairs):
            copy = remote(src, buf, me, d, j, ahead(d))
            copy.start()
            started.append(copy)
    for j, (src, buf) in enumerate(pairs):
        copy = remote(src, buf, me, 0, j, sibling)
        copy.start()
        started.append(copy)

    rows_at = lax.broadcasted_iota(jnp.int32, (SPAN, SPAN), 0)
    cols_at = lax.broadcasted_iota(jnp.int32, (SPAN, SPAN), 1)
    eye = jnp.where(rows_at == cols_at, 1.0, 0.0).astype(jnp.bfloat16)
    vone[:, DH:] = jnp.ones((wide, DH), jnp.bfloat16)

    def chunk(d, first):
        owner = (chip + chips - d) % chips
        begin = owner * 2 * spans
        for t in range(2 * spans):
            place = pl.ds(t * SPAN, SPAN)
            piece = kbuf[begin + t]
            vone[place, :DH] = vbuf[begin + t]
            for i in range(spans):
                gap = (table_ref[me * spans + i] - table_ref[begin + t]) * SPAN
                kmask[i, place, :DH] = piece
                kmask[i, place, DH:] = jnp.where(rows_at - cols_at > gap, HIDE, 0.0).astype(
                    jnp.bfloat16
                )

        def attend_group(g):
            for i in range(spans):
                lines = pl.ds(i * SPAN, SPAN)
                query = jnp.concatenate(
                    [
                        jnp.concatenate(
                            [
                                q_ref[lines, pl.ds(pl.multiple_of((g * per + h) * DH, DH), DH)],
                                eye,
                            ],
                            axis=1,
                        )
                        for h in range(per)
                    ],
                    axis=0,
                )
                score = lax.dot_general(
                    query, kmask[i], (((1,), (1,)), ((), ())), preferred_element_type=jnp.float32
                )
                high = jnp.broadcast_to(jnp.max(score, axis=1, keepdims=True), (size, DH))
                if not first:
                    old = top[g, i]
                    high = jnp.maximum(high, old)
                weight = jnp.concatenate(
                    [
                        jnp.exp2((score[:, t * SPAN : (t + 1) * SPAN] - high) * rate).astype(
                            jnp.bfloat16
                        )
                        for t in range(2 * spans)
                    ],
                    axis=1,
                )
                update = jnp.dot(weight, vone[...], preferred_element_type=jnp.float32)
                top[g, i] = high
                if first:
                    acc[g, i] = update
                else:
                    factor = jnp.exp2((old - high) * rate)
                    acc[g, i, :, :DH] = acc[g, i, :, :DH] * factor + update[:, :DH]
                    acc[g, i, :, DH:] = acc[g, i, :, DH:] * factor + update[:, DH:]

        return lambda: pl.loop(0, groups)(attend_group)

    for copy in local:
        copy.wait()
    for j, (src, buf) in enumerate(pairs):
        remote(src, buf, sibling, 0, j, sibling).wait_recv()
    chunk(0, True)()

    for d in range(1, chips):
        for j, (src, buf) in enumerate(pairs):
            origin = behind(d, core)
            remote(src, buf, origin, d, j, sibling).wait_recv()
            copy = remote(slot(buf, origin), buf, origin, chips - 1 + d, j, sibling)
            copy.start()
            started.append(copy)
    for d in range(1, chips):
        for j, (src, buf) in enumerate(pairs):
            remote(src, buf, behind(d, 1 - core), chips - 1 + d, j, sibling).wait_recv()

    for s in range(spans):
        wanted = jnp.int32(0)
        for p in range(slots_ref.shape[0]):
            wanted = jnp.where(slots_ref[p] == me * spans + s, p, wanted)
        for j, buf in enumerate((kbuf, vbuf)):
            raw = buf[wanted].astype(jnp.float32)
            level = jnp.max(jnp.max(jnp.abs(raw), axis=0, keepdims=True), axis=1, keepdims=True)
            level = level + 1e-06
            cache_ref[page, s, j] = (raw / level).astype(jnp.bfloat16)
            scales_ref[page, s, j] = jnp.broadcast_to(level, (8, DH))

    def pages(index, target):
        return [
            pltpu.make_async_remote_copy(
                src_ref=ref.at[page],
                dst_ref=ref.at[page],
                send_sem=page_send.at[index, j],
                recv_sem=page_recv.at[index, j],
                device_id={"page": target},
                device_id_type=MESH,
            )
            for j, ref in enumerate((cache_ref, scales_ref))
        ]

    def arrived(index):
        origin = (page + n_page - index) % n_page
        for j, ref in enumerate((cache_ref, scales_ref)):
            pltpu.make_async_remote_copy(
                src_ref=ref.at[origin],
                dst_ref=ref.at[origin],
                send_sem=page_send.at[index, j],
                recv_sem=page_recv.at[index, j],
                device_id={"page": (page + index) % n_page},
                device_id_type=MESH,
            ).wait_recv()

    for d in range(1, chips):
        attend = chunk(d, False)
        if d == 1:
            for index in range(1, n_page):
                for copy in pages(index, (page + index) % n_page):
                    copy.start()
                    started.append(copy)
        attend()

    @pl.loop(0, groups)
    def _(g):
        for i in range(spans):
            for h in range(per):
                lines = pl.ds(h * SPAN, SPAN)
                out_ref[
                    pl.ds(i * SPAN, SPAN), pl.ds(pl.multiple_of((g * per + h) * DH, DH), DH)
                ] = (acc[g, i, lines, :DH] / acc[g, i, lines, DH:]).astype(jnp.bfloat16)

    for index in range(1, n_page):
        arrived(index)
    for copy in started:
        copy.wait_send()


def on_device(n, n_page, queries, keys, values, span_table, page_slots):
    rows = queries.shape[0]
    heads = queries.shape[1] // DH
    spans = rows // SPAN
    per = math.gcd(heads, 4)
    groups = heads // per
    chips = n // 2
    wide = 2 * rows
    vmem = pl.BlockSpec(memory_space=pltpu.VMEM)
    hbm = pl.BlockSpec(memory_space=pltpu.HBM)
    attended, cache, scales = pl.pallas_call(
        functools.partial(kernel, n, n_page, heads),
        out_shape=(
            jax.ShapeDtypeStruct((rows, heads * DH), jnp.bfloat16),
            jax.ShapeDtypeStruct((n_page, spans, 2, PAGE, DH), jnp.bfloat16),
            jax.ShapeDtypeStruct((n_page, spans, 2, 8, DH), jnp.float32),
        ),
        in_specs=[hbm] * 5,
        out_specs=(vmem, vmem, vmem),
        scratch_shapes=[
            pltpu.SMEM(span_table.shape, jnp.int32),
            pltpu.SMEM(page_slots.shape, jnp.int32),
            pltpu.VMEM(queries.shape, jnp.bfloat16),
            pltpu.VMEM((n * spans, SPAN, DH), jnp.bfloat16),
            pltpu.VMEM((n * spans, SPAN, DH), jnp.bfloat16),
            pltpu.VMEM((spans, wide, 2 * DH), jnp.bfloat16),
            pltpu.VMEM((wide, 2 * DH), jnp.bfloat16),
            pltpu.VMEM((groups, spans, per * SPAN, 2 * DH), jnp.float32),
            pltpu.VMEM((groups, spans, per * SPAN, DH), jnp.float32),
            pltpu.SemaphoreType.DMA((n, 2)),
            pltpu.SemaphoreType.DMA((n, 2)),
            pltpu.SemaphoreType.DMA((5,)),
            pltpu.SemaphoreType.DMA((n_page, 2)),
            pltpu.SemaphoreType.DMA((n_page, 2)),
        ],
        compiler_params=pltpu.CompilerParams(
            collective_id=0, has_side_effects=True, vmem_limit_bytes=67043328
        ),
    )(
        span_table,
        page_slots,
        queries,
        keys.reshape(spans, SPAN, DH),
        values.reshape(spans, SPAN, DH),
    )
    cache = cache.transpose(1, 0, 2, 3, 4)
    scales = scales[:, :, :, 0, 0].transpose(1, 0, 2)
    return attended, cache, scales


def solution(mesh):
    placed = (P("ctx", "page"), P("ctx", "page"), P("ctx", "page"), P(), P())
    return jax.shard_map(
        functools.partial(on_device, mesh.shape["ctx"], mesh.shape["page"]),
        mesh=mesh,
        in_specs=placed,
        out_specs=(P("ctx", "page"), P("ctx", None, None, None, None), P("ctx", None, None)),
        check_vma=False,
    )
```

profile of v0, /device:TPU:1, one launch (start us, length us, event | category | flops | bytes accessed | tf_op | source)
XLA Modules:
  0.0 34.5 jit_solution(4315890753491343187)
XLA Ops:
  0.6 29.4 %shard_map.76 = (bf16[256,2048]{1,0:T(8,128)(2,1)}, bf16[4,2,2,128,128]{4,3,2,1,0:T(8,128)(2,1)}, f32[4,2,2,8,128]{4,3,2,1,0:T(8,128)}) custom-call(s32[16]{0:T(128)} %table_in.1, s32[16]{0:T(128)} %slots_in.1, bf16[256,2048]{1,0:T(8,128)(2,1)} %q_in.1, bf16[2,128,128]{2,1,0:T(8,128)(2,1)} %bitcast.7, bf16[2,128,128]{2,1,0:T(8,128)(2,1)} %bitcast.8), custom_call_target="tpu_custom_call" | custom-call | tf_op jit(solution)/shard_map/pallas_call | solution.py:240
  30.1 0.0 copy-start
  30.1 2.0 %copy.9 = bf16[2,4,2,128,128]{4,3,2,1,0:T(8,128)(2,1)} copy(bf16[2,4,2,128,128]{4,3,2,0,1:T(8,128)(2,1)} %bitcast.6) | data formatting | bytes 1048576
  32.0 0.8 %slice.3 = f32[4,2,2,1,1]{4,3,2,1,0:T(1,128)S(1)} slice(f32[4,2,2,8,128]{4,3,2,1,0:T(8,128)} %get-tuple-element.8), slice={[0:4], [0:2], [0:2], [0:1], [0:1]} | slice | bytes 128 | tf_op jit(solution)/shard_map/slice | solution.py:276
  32.9 0.7 %copy.8 = f32[4,2,2,1,1]{0,2,4,3,1:T(2,128)} copy(f32[4,2,2,1,1]{4,3,2,1,0:T(1,128)S(1)} %slice.3) | data formatting | bytes 128 | tf_op jit(solution)/shard_map/slice | solution.py:276
  33.6 0.0 copy-done
  33.6 1.0 %copy.11 = bf16[256,2048]{1,0:T(8,128)(2,1)} copy(bf16[256,2048]{1,0:T(8,128)(2,1)S(1)} %copy-done) | data formatting | bytes 2097152
Async XLA Ops:
  30.1 3.5 %copy-start = (bf16[256,2048]{1,0:T(8,128)(2,1)S(1)}, bf16[256,2048]{1,0:T(8,128)(2,1)}, u32[]{:S(2)}) copy-start(bf16[256,2048]{1,0:T(8,128)(2,1)} %get-tuple-element.15) | copy-start | bytes 3145732
where the time goes:
time: 34.7 us; the launch traced here: 34.5 us
  Pallas kernels  29.4 us (85%)
  local copies, waits for them, and re-layouts  4.47 us (13%)
  between operations  0.65 us (2%)
    pallas_call x1, Pallas kernels, on_device(): pl.pallas_call(functools.partial(kernel, n, n_page, heads), out_shape=(ja...  29.4 us
    unnamed x4, local copies, waits for them, and re-layouts  2.95 us
    slice x2, local copies, waits for them, and re-layouts, on_device(): scales = scales[:, :, :, 0, 0].transpose(1, 0, 2)  1.53 us

commit v1 on v0

v1 whole, which is shorter than its diff:
```python
import functools
import math

import jax
import jax.numpy as jnp
from jax import lax
from jax.experimental import pallas as pl
from jax.experimental.pallas import tpu as pltpu
from jax.sharding import PartitionSpec as P

DH = 128
PAGE = 128
SPAN = 128
HIDE = -1e30
PAIR = 2
PIECES = (32, 32, 32, 32)
MESH = pl.DeviceIdType.MESH


def kernel(
    n, n_page, heads, spans, table_in, slots_in, q_in, k_in, v_in,
    att_out, cache_out, scales_out,
    table_ref, slots_ref, bias, own_bias, q_ref, own, qs, kc, vt, s0, s1, p0, p1,
    tops, acc, att, cache, scales, send, recv, own_sem, page_send, page_recv, out_sem,
    *pieces,
):
    count = len(PIECES)
    bufs, zbufs = pieces[:count], pieces[count:]
    starts = [sum(PIECES[:p]) for p in range(count)]
    chips = n // 2
    pairs = heads // PAIR
    wide = PAIR * SPAN
    units = pairs * spans
    me = lax.axis_index("ctx")
    page = lax.axis_index("page")
    chip = me // 2
    core = me % 2
    sibling = 2 * chip + 1 - core
    rate = DH ** (-0.5) * math.log2(math.e)

    def ahead(d):
        return 2 * ((chip + d) % chips) + core

    def behind(d, c):
        return 2 * ((chip + chips - d) % chips) + c

    barrier = pltpu.get_barrier_semaphore()
    for d in range(1, chips):
        pl.semaphore_signal(barrier, inc=1, device_id={"ctx": ahead(d)}, device_id_type=MESH)
    pl.semaphore_signal(barrier, inc=1, device_id={"ctx": sibling}, device_id_type=MESH)
    for d in range(1, n_page):
        pl.semaphore_signal(
            barrier, inc=1, device_id={"page": (page + d) % n_page}, device_id_type=MESH
        )

    local = []

    def fetch(src, dst, j):
        copy = pltpu.make_async_copy(src, dst, own_sem.at[j])
        copy.start()
        local.append(copy)

    fetch(q_in, q_ref, 0)
    fetch(k_in, own.at[0], 1)
    fetch(v_in, own.at[1], 2)
    fetch(table_in, table_ref, 3)
    fetch(slots_in, slots_ref, 4)

    rows_at = lax.broadcasted_iota(jnp.int32, (SPAN, wide), 1) % SPAN
    keys_at = lax.broadcasted_iota(jnp.int32, (SPAN, wide), 0)
    vt[DH:, :] = jnp.ones((vt.shape[0] - DH, vt.shape[1]), jnp.bfloat16)
    for copy in local:
        copy.wait()
    mine = []
    for p in range(count):
        copy = pltpu.make_async_copy(
            own.at[:, :, pl.ds(starts[p], PIECES[p])], bufs[p].at[me], own_sem.at[5 + p]
        )
        copy.start()
        mine.append(copy)

    for i in range(spans):
        here = table_ref[me * spans + i]
        for t in range(spans):
            own_bias[i * spans + t] = jnp.where(table_ref[me * spans + t] < here, 0.0, HIDE)
        for d in range(1, n):
            for t in range(spans):
                there = table_ref[((me + d) % n) * spans + t]
                bias[(i * (n - 1) + d - 1) * spans + t] = jnp.where(there < here, 0.0, HIDE)

    @pl.loop(0, pairs)
    def _(g):
        for i in range(spans):
            for h in range(PAIR):
                place = pl.ds(pl.multiple_of((g * PAIR + h) * DH, DH), DH)
                value = q_ref[pl.ds(i * SPAN, SPAN), place].astype(jnp.float32) * rate
                high = value.astype(jnp.bfloat16)
                qs[g * spans + i, h * SPAN : (h + 1) * SPAN, :DH] = high
                qs[g * spans + i, h * SPAN : (h + 1) * SPAN, DH:] = (
                    value - high.astype(jnp.float32)
                ).astype(jnp.bfloat16)

    def attention(size, rows, first):
        blocks = size // rows
        steps = rows // 8

        def shift(i, t):
            return own_bias[i * spans + t] if first else bias[i * blocks + t]

        def score(u, i, s):
            keys = kc[:size]
            value = lax.dot_general(
                jnp.concatenate([keys, keys], axis=1), qs[u],
                (((1,), (1,)), ((), ())), preferred_element_type=jnp.float32,
            )
            best = None
            for t in range(blocks):
                part = value[t * rows : (t + 1) * rows]
                if first and t == i:
                    part = jnp.where(keys_at > rows_at, HIDE, part)
                s[t * rows : (t + 1) * rows] = part
                high = part[:8]
                for r in range(1, steps):
                    high = jnp.maximum(high, part[r * 8 : (r + 1) * 8])
                if not (first and t == i):
                    high = high + shift(i, t)
                best = high if best is None else jnp.maximum(best, high)
            best = jnp.broadcast_to(jnp.max(best, axis=0, keepdims=True), (8, wide))
            if first:
                tops[u] = best
                return best, best
            old = tops[u]
            new = jnp.maximum(old, best)
            tops[u] = new
            return new, jnp.exp2(old - new)

        def weigh(i, high, s, w):
            for t in range(blocks):
                level = high if first and t == i else high - shift(i, t)
                level = jnp.concatenate([level] * steps, axis=0)
                w[t * rows : (t + 1) * rows] = jnp.exp2(
                    s[t * rows : (t + 1) * rows] - level
                ).astype(jnp.bfloat16)

        def gather(u, factor, w):
            update = jnp.dot(vt[:, :size], w[:size], preferred_element_type=jnp.float32)
            update = update[: DH + 8]
            if first:
                acc[u] = update
            else:
                acc[u] = acc[u] * jnp.concatenate([factor] * (DH // 8 + 1), axis=0) + update

        per = math.gcd(pairs, max(1, 8 * 512 // (spans * size))) * spans
        ss, ww = (s0, s1), (p0, p1)

        def body(j, carry):
            (high, factor), late = carry
            for x in range(per):
                u = per * j + x
                now = x % 2
                weigh(x % spans, high, ss[now], ww[now])
                after = score((u + 1) % units, (x + 1) % spans, ss[1 - now])
                before = u - 1 if x else lax.rem(u + units, units + 1)
                gather(before, late, ww[1 - now])
                late = factor
                high, factor = after
            return (high, factor), late

        start = score(0, 0, s0)
        carry = lax.fori_loop(0, units // per, body, (start, start[1]))
        gather(units - 1, carry[1], ww[(per - 1) % 2])

    size = spans * SPAN
    kc[:size] = own[0].reshape(size, DH)
    vt[:DH, :size] = own[1].reshape(size, DH).T
    attention(size, SPAN, True)

    pl.semaphore_wait(barrier, chips + n_page - 1)

    def remote(p, src, owner, index, target):
        return pltpu.make_async_remote_copy(
            src_ref=src,
            dst_ref=bufs[p].at[owner],
            send_sem=send.at[p, index],
            recv_sem=recv.at[p, index],
            device_id={"ctx": target},
            device_id_type=MESH,
        )

    started = []
    for p in range(count):
        part = own.at[:, :, pl.ds(starts[p], PIECES[p])]
        for d in range(1, chips):
            copy = remote(p, part, me, d, ahead(d))
            copy.start()
            started.append(copy)
        copy = remote(p, part, me, 0, sibling)
        copy.start()
        started.append(copy)

    wanted = []
    for s in range(spans):
        device, place = jnp.int32(0), jnp.int32(0)
        for g in range(n * spans):
            hit = slots_ref[g] == me * spans + s
            device = jnp.where(hit, g // spans, device)
            place = jnp.where(hit, g % spans, place)
        wanted.append((device, place))

    def collect(p):
        buf = bufs[p]
        for d in range(1, chips):
            origin = behind(d, core)
            remote(p, buf.at[origin], origin, d, sibling).wait_recv()
            copy = remote(p, buf.at[origin], origin, chips - 1 + d, sibling)
            copy.start()
            started.append(copy)
        mine[p].wait()
        remote(p, buf.at[sibling], sibling, 0, sibling).wait_recv()
        for d in range(1, chips):
            origin = behind(d, 1 - core)
            remote(p, buf.at[origin], origin, chips - 1 + d, sibling).wait_recv()

    def page_copy(p, index, target, origin):
        ref = zbufs[p].at[origin]
        return pltpu.make_async_remote_copy(
            src_ref=ref,
            dst_ref=ref,
            send_sem=page_send.at[p, index],
            recv_sem=page_recv.at[p, index],
            device_id={"page": target},
            device_id_type=MESH,
        )

    def select(p):
        for s in range(spans):
            device, place = wanted[s]
            for j in range(2):
                zbufs[p][page, j, s] = bufs[p][device, j, place]

    def publish(p):
        for index in range(1, n_page):
            copy = page_copy(p, index, (page + index) % n_page, page)
            copy.start()
            started.append(copy)

    for p in range(count):
        rows = PIECES[p]
        size = (n - 1) * spans * rows
        collect(p)
        select(p)
        other = []
        for d in range(1, n):
            for t in range(spans):
                place = ((d - 1) * spans + t) * rows
                kc[place : place + rows] = bufs[p][(me + d) % n, 0, t]
                other.append(bufs[p][(me + d) % n, 1, t])
        publish(p)
        vt[:DH, :size] = jnp.concatenate(other, axis=0).T
        attention(size, rows, False)

    @pl.loop(0, pairs)
    def _(g):
        for i in range(spans):
            u = g * spans + i
            total = jnp.concatenate([acc[u, DH : DH + 8]] * (DH // 8), axis=0)
            value = (acc[u, :DH] / total).T
            for h in range(PAIR):
                place = pl.ds(pl.multiple_of((g * PAIR + h) * DH, DH), DH)
                att[pl.ds(i * SPAN, SPAN), place] = value[h * SPAN : (h + 1) * SPAN].astype(
                    jnp.bfloat16
                )

    finish = pltpu.make_async_copy(att, att_out, out_sem.at[0])
    finish.start()

    for p in range(count):
        for index in range(1, n_page):
            origin = (page + n_page - index) % n_page
            page_copy(p, index, page, origin).wait_recv()

    lanes = lax.broadcasted_iota(jnp.int32, (8, DH), 1)
    for s in range(spans):
        for j in range(2):
            levels = jnp.zeros((8, DH), jnp.float32)
            for h in range(n_page):
                level = None
                for p in range(count):
                    high = jnp.max(jnp.abs(zbufs[p][h, j, s].astype(jnp.float32)), axis=0, keepdims=True)
                    level = high if level is None else jnp.maximum(level, high)
                level = jnp.max(level, axis=1, keepdims=True) + 1e-06
                for p in range(count):
                    cache[s, h, j, starts[p] : starts[p] + PIECES[p]] = (
                        zbufs[p][h, j, s].astype(jnp.float32) / level
                    ).astype(jnp.bfloat16)
                levels = jnp.where(lanes == h, level, levels)
            scales[s, j] = levels
    last = [
        pltpu.make_async_copy(cache, cache_out, out_sem.at[1]),
        pltpu.make_async_copy(scales, scales_out, out_sem.at[2]),
    ]
    for copy in last:
        copy.start()
    for copy in started:
        copy.wait_send()
    finish.wait()
    for copy in last:
        copy.wait()


def place_results(att_in, cache_in, scales_in, att_out, cache_out, scales_out, att, cache, sems):
    parts = 4
    rows = att.shape[0] // parts
    moves = []
    for j in range(parts):
        place = pl.ds(j * rows, rows)
        moves.append((att_in.at[place], att.at[place], att_out.at[place]))
    for s in range(cache.shape[0]):
        moves.append((cache_in.at[s], cache.at[s], cache_out.at[s]))
    ins = [pltpu.make_async_copy(a, b, sems.at[0, j]) for j, (a, b, _) in enumerate(moves)]
    outs = [pltpu.make_async_copy(b, c, sems.at[1, j]) for j, (_, b, c) in enumerate(moves)]
    for copy in ins:
        copy.start()
    for s in range(scales_out.shape[0]):
        for j in range(scales_out.shape[1]):
            scales_out[s, j : j + 1] = scales_in[s, j, :1, : scales_out.shape[2]]
    for a, b in zip(ins, outs):
        a.wait()
        b.start()
    for copy in outs:
        copy.wait()


def on_device(n, n_page, queries, keys, values, span_table, page_slots):
    rows = queries.shape[0]
    heads = queries.shape[1] // DH
    spans = rows // SPAN
    units = heads // PAIR * spans
    wide = PAIR * SPAN
    most = max(spans * SPAN, max((n - 1) * spans * p for p in PIECES))
    padded = -(-most // 128) * 128
    any_space = pl.BlockSpec(memory_space=pl.ANY)
    vmem = pl.BlockSpec(memory_space=pltpu.VMEM)
    count = len(PIECES)
    results = (
        jax.ShapeDtypeStruct((rows, heads * DH), jnp.bfloat16),
        jax.ShapeDtypeStruct((spans, n_page, 2, PAGE, DH), jnp.bfloat16),
        jax.ShapeDtypeStruct((spans, 2, 8, DH), jnp.float32),
    )
    attended, cache, scales = pl.pallas_call(
        functools.partial(kernel, n, n_page, heads, spans),
        out_shape=results,
        in_specs=[any_space] * 5,
        out_specs=(any_space,) * 3,
        scratch_shapes=[
            pltpu.SMEM(span_table.shape, jnp.int32),
            pltpu.SMEM(page_slots.shape, jnp.int32),
            pltpu.SMEM((spans * (n - 1) * spans,), jnp.float32),
            pltpu.SMEM((spans * spans,), jnp.float32),
            pltpu.VMEM(queries.shape, jnp.bfloat16),
            pltpu.VMEM((2, spans, SPAN, DH), jnp.bfloat16),
            pltpu.VMEM((units, wide, 2 * DH), jnp.bfloat16),
            pltpu.VMEM((most, DH), jnp.bfloat16),
            pltpu.VMEM((DH + 16, padded), jnp.bfloat16),
            pltpu.VMEM((most, wide), jnp.float32),
            pltpu.VMEM((most, wide), jnp.float32),
            pltpu.VMEM((most, wide), jnp.bfloat16),
            pltpu.VMEM((most, wide), jnp.bfloat16),
            pltpu.VMEM((units, 8, wide), jnp.float32),
            pltpu.VMEM((units + 1, DH + 8, wide), jnp.float32),
            pltpu.VMEM(queries.shape, jnp.bfloat16),
            pltpu.VMEM((spans, n_page, 2, PAGE, DH), jnp.bfloat16),
            pltpu.VMEM((spans, 2, 8, DH), jnp.float32),
            pltpu.SemaphoreType.DMA((count, n)),
            pltpu.SemaphoreType.DMA((count, n)),
            pltpu.SemaphoreType.DMA((5 + count,)),
            pltpu.SemaphoreType.DMA((count, n_page)),
            pltpu.SemaphoreType.DMA((count, n_page)),
            pltpu.SemaphoreType.DMA((3,)),
        ]
        + [pltpu.VMEM((n, 2, spans, p, DH), jnp.bfloat16) for p in PIECES]
        + [pltpu.VMEM((n_page, 2, spans, p, DH), jnp.bfloat16) for p in PIECES],
        compiler_params=pltpu.CompilerParams(
            collective_id=0, has_side_effects=True, vmem_limit_bytes=48 * 2**20
        ),
    )(
        span_table,
        page_slots,
        queries,
        keys.reshape(spans, SPAN, DH),
        values.reshape(spans, SPAN, DH),
    )
    attended, cache, scales = pl.pallas_call(
        place_results,
        out_shape=results[:2] + (jax.ShapeDtypeStruct((spans, 2, n_page), jnp.float32),),
        in_specs=[any_space, any_space, vmem],
        out_specs=(any_space, any_space, vmem),
        scratch_shapes=[
            pltpu.VMEM((rows, heads * DH), jnp.bfloat16),
            pltpu.VMEM((spans, n_page, 2, PAGE, DH), jnp.bfloat16),
            pltpu.SemaphoreType.DMA((2, 4 + spans)),
        ],
        compiler_params=pltpu.CompilerParams(vmem_limit_bytes=16 * 2**20),
    )(attended, cache, scales)
    return attended, cache, scales.transpose(0, 2, 1)


def solution(mesh):
    placed = (P("ctx", "page"), P("ctx", "page"), P("ctx", "page"), P(), P())
    return jax.shard_map(
        functools.partial(on_device, mesh.shape["ctx"], mesh.shape["page"]),
        mesh=mesh,
        in_specs=placed,
        out_specs=(P("ctx", "page"), P("ctx", None, None, None, None), P("ctx", None, None)),
        check_vma=False,
    )
```

time: 34.7 us -> 36.2 us (1.043)
  the two profiles are of different devices: /device:TPU:1 before, /device:TPU:0 now
where the time goes in v1:
time: 36.2 us; the launch traced here: 35.9 us
  Pallas kernels  31.7 us (88%)
  local copies, waits for them, and re-layouts  3.56 us (10%)
  between operations  0.66 us (2%)
    pallas_call x1, Pallas kernels, on_device(): pl.pallas_call(functools.partial(kernel, n, n_page, heads, spans), out_sh...  29.8 us
    unnamed x10, local copies, waits for them, and re-layouts  3.56 us
    pallas_call x1, Pallas kernels, on_device(): pl.pallas_call(place_results, out_shape=results[:2] + (jax.ShapeDtypeStru...  1.93 us

profile of v1, /device:TPU:0, one launch (start us, length us, event | category | flops | bytes accessed | tf_op | source)
XLA Modules:
  0.0 35.9 jit_solution(15608461786276672793)
XLA Ops:
  0.6 0.0 copy-start.3
  0.6 0.0 copy-start.4
  0.7 0.6 %copy-done.3 = s32[16]{0:T(128)S(1)} copy-done((s32[16]{0:T(128)S(1)}, s32[16]{0:T(128)}, u32[]{:S(2)}) %copy-start.3) | copy-done | bytes 88
  1.3 0.0 copy-done.4
  1.3 0.0 copy-start
  1.3 1.2 %copy-done = bf16[256,2048]{1,0:T(8,128)(2,1)S(1)} copy-done((bf16[256,2048]{1,0:T(8,128)(2,1)S(1)}, bf16[256,2048]{1,0:T(8,128)(2,1)}, u32[]{:S(2)}) %copy-start) | copy-done | bytes 1048600
  2.5 0.0 copy-start.1
  2.5 0.8 %copy-done.1 = bf16[256,128]{1,0:T(8,128)(2,1)S(1)} copy-done((bf16[256,128]{1,0:T(8,128)(2,1)S(1)}, bf16[256,128]{1,0:T(8,128)(2,1)}, u32[]{:S(2)}) %copy-start.1) | copy-done | bytes 65560
  3.4 0.0 copy-start.2
  3.4 0.8 %copy-done.2 = bf16[256,128]{1,0:T(8,128)(2,1)S(1)} copy-done((bf16[256,128]{1,0:T(8,128)(2,1)S(1)}, bf16[256,128]{1,0:T(8,128)(2,1)}, u32[]{:S(2)}) %copy-start.2) | copy-done | bytes 65560
  4.2 29.8 %shard_map.76 = (bf16[256,2048]{1,0:T(8,128)(2,1)S(1)}, bf16[2,4,2,128,128]{4,3,2,1,0:T(8,128)(2,1)S(1)}, f32[2,2,8,128]{3,2,1,0:T(8,128)S(1)}) custom-call(s32[16]{0:T(128)S(1)} %copy-done.3, s32[16]{0:T(128)S(1)} %copy-done.4, bf16[256,2048]{1,0:T(8,128)(2,1)S(1)} %copy-done, bf16[2,128,128]{2,1,0:T(8,128)(2,1)S(1)} %bitcast.3, ...), custom_call_target="tpu_custom_call" | custom-call | tf_op jit(solution)/shard_map/pallas_call | solution.py:350
  34.0 1.9 %shard_map.77 = (bf16[256,2048]{1,0:T(8,128)(2,1)}, bf16[2,4,2,128,128]{4,3,2,1,0:T(8,128)(2,1)}, f32[2,2,4]{2,1,0:T(2,128)}) custom-call(bf16[256,2048]{1,0:T(8,128)(2,1)S(1)} %get-tuple-element.9.att_in, bf16[2,4,2,128,128]{4,3,2,1,0:T(8,128)(2,1)S(1)} %get-tuple-element.10.cache_in, f32[2,2,8,128]{3,2,1,0:T(8,128)S(1)} %get-tuple-element.11.scales_in), custom_call_target="tpu_custom_call" | custom-call | tf_op jit(solution)/shard_map/pallas_call | solution.py:393
Async XLA Ops:
  0.6 0.7 %copy-start.3 = (s32[16]{0:T(128)S(1)}, s32[16]{0:T(128)}, u32[]{:S(2)}) copy-start(s32[16]{0:T(128)} %table_in.1) | copy-start | bytes 196
  0.6 0.7 %copy-start.4 = (s32[16]{0:T(128)S(1)}, s32[16]{0:T(128)}, u32[]{:S(2)}) copy-start(s32[16]{0:T(128)} %slots_in.1) | copy-start | bytes 196
  1.3 1.2 %copy-start = (bf16[256,2048]{1,0:T(8,128)(2,1)S(1)}, bf16[256,2048]{1,0:T(8,128)(2,1)}, u32[]{:S(2)}) copy-start(bf16[256,2048]{1,0:T(8,128)(2,1)} %q_in.1) | copy-start | bytes 3145732
  2.5 0.8 %copy-start.1 = (bf16[256,128]{1,0:T(8,128)(2,1)S(1)}, bf16[256,128]{1,0:T(8,128)(2,1)}, u32[]{:S(2)}) copy-start(bf16[256,128]{1,0:T(8,128)(2,1)} %param.6) | copy-start | bytes 196612
  3.4 0.8 %copy-start.2 = (bf16[256,128]{1,0:T(8,128)(2,1)S(1)}, bf16[256,128]{1,0:T(8,128)(2,1)}, u32[]{:S(2)}) copy-start(bf16[256,128]{1,0:T(8,128)(2,1)} %param.7) | copy-start | bytes 196612

commit v2 on v1

v2 whole, which is shorter than its diff:
```python
import functools
import math

import jax
import jax.numpy as jnp
from jax import lax
from jax.experimental import pallas as pl
from jax.experimental.pallas import tpu as pltpu
from jax.sharding import PartitionSpec as P

DH = 128
PAGE = 128
SPAN = 128
HIDE = -1e30
PAIR = 2
PIECES = (32, 32, 32, 32)
MESH = pl.DeviceIdType.MESH


def kernel(
    n, n_page, heads, spans, table_in, slots_in, q_in, k_in, v_in,
    att_out, cache_out, scales_out,
    table_ref, slots_ref, bias, q_ref, own, vts, s0, s1, p0, p1,
    tops, acc, att, cache, scales, send, recv, own_sem, page_send, page_recv, out_sem,
    *pieces,
):
    count = len(PIECES)
    bufs, zbufs = pieces[:count], pieces[count:]
    starts = [sum(PIECES[:p]) for p in range(count)]
    chips = n // 2
    pairs = heads // PAIR
    wide = PAIR * SPAN
    units = pairs * spans
    me = lax.axis_index("ctx")
    page = lax.axis_index("page")
    chip = me // 2
    core = me % 2
    sibling = 2 * chip + 1 - core
    rate = DH ** (-0.5) * math.log2(math.e)

    def ahead(d):
        return 2 * ((chip + d) % chips) + core

    def behind(d, c):
        return 2 * ((chip + chips - d) % chips) + c

    barrier = pltpu.get_barrier_semaphore()
    for d in range(1, chips):
        pl.semaphore_signal(barrier, inc=1, device_id={"ctx": ahead(d)}, device_id_type=MESH)
    pl.semaphore_signal(barrier, inc=1, device_id={"ctx": sibling}, device_id_type=MESH)
    for d in range(1, n_page):
        pl.semaphore_signal(
            barrier, inc=1, device_id={"page": (page + d) % n_page}, device_id_type=MESH
        )

    local = []

    def fetch(src, dst, j):
        copy = pltpu.make_async_copy(src, dst, own_sem.at[j])
        copy.start()
        local.append(copy)

    fetch(q_in, q_ref, 0)
    fetch(k_in, own.at[0], 1)
    fetch(v_in, own.at[1], 2)
    fetch(table_in, table_ref, 3)
    fetch(slots_in, slots_ref, 4)

    rows_at = lax.broadcasted_iota(jnp.int32, (SPAN, wide), 1) % SPAN
    keys_at = lax.broadcasted_iota(jnp.int32, (SPAN, wide), 0)
    for vt in vts:
        vt[DH:, :] = jnp.ones((vt.shape[0] - DH, vt.shape[1]), jnp.bfloat16)
    for copy in local:
        copy.wait()
    mine = []
    for p in range(count):
        copy = pltpu.make_async_copy(
            own.at[:, :, pl.ds(starts[p], PIECES[p])], bufs[p].at[me], own_sem.at[5 + p]
        )
        copy.start()
        mine.append(copy)

    order = [me, sibling]
    for d in range(1, chips):
        order += [behind(d, core), behind(d, 1 - core)]
    for i in range(spans):
        here = table_ref[me * spans + i]
        for d, device in enumerate(order):
            for t in range(spans):
                there = table_ref[device * spans + t]
                bias[(i * n + d) * spans + t] = jnp.where(there < here, 0.0, HIDE)

    class Chunk:
        def __init__(self, parts, rows, base, vt, diagonal):
            self.parts = parts
            self.rows = rows
            self.base = base
            self.vt = vt
            self.diagonal = diagonal
            self.blocks = len(parts) * spans
            self.size = self.blocks * rows

        def stage(self):
            other = [part(1, t) for part in self.parts for t in range(spans)]
            self.vt[:DH, : self.size] = jnp.concatenate(other, axis=0).T

        def keys(self):
            return jnp.concatenate(
                [part(0, t) for part in self.parts for t in range(spans)], axis=0
            )

        def shift(self, i, t):
            if self.diagonal and t == i:
                return None
            return bias[i * n * spans + self.base * spans + t]

    def pair_of(u, i):
        return (u - i) // spans if isinstance(u, int) else lax.div(u - i, spans)

    def score(chunk, u, i, s):
        g = pair_of(u, i)
        query = jnp.concatenate(
            [
                q_ref[
                    pl.ds(i * SPAN, SPAN),
                    pl.ds(pl.multiple_of((g * PAIR + h) * DH, DH), DH),
                ]
                for h in range(PAIR)
            ],
            axis=0,
        )
        value = lax.dot_general(
            chunk.keys(), query, (((1,), (1,)), ((), ())), preferred_element_type=jnp.float32
        )
        best = None
        rows = chunk.rows
        for t in range(chunk.blocks):
            part = value[t * rows : (t + 1) * rows]
            offset = chunk.shift(i, t)
            if offset is None:
                part = jnp.where(keys_at > rows_at, HIDE, part)
            s[t * rows : (t + 1) * rows] = part
            high = part[:8]
            for r in range(1, rows // 8):
                high = jnp.maximum(high, part[r * 8 : (r + 1) * 8])
            if offset is not None:
                high = high + offset
            best = high if best is None else jnp.maximum(best, high)
        best = jnp.broadcast_to(jnp.max(best, axis=0, keepdims=True), (8, wide))
        if chunk.diagonal:
            tops[u] = best
            return best, best
        old = tops[u]
        new = jnp.maximum(old, best)
        tops[u] = new
        return new, jnp.exp2((old - new) * rate)

    def weigh(chunk, i, high, s, w):
        rows = chunk.rows
        for t in range(chunk.blocks):
            offset = chunk.shift(i, t)
            level = high if offset is None else high - offset
            level = jnp.concatenate([level] * (rows // 8), axis=0)
            w[t * rows : (t + 1) * rows] = jnp.exp2(
                (s[t * rows : (t + 1) * rows] - level) * rate
            ).astype(jnp.bfloat16)

    def gather(chunk, u, factor, w):
        update = jnp.dot(
            chunk.vt[:, : chunk.size], w[: chunk.size], preferred_element_type=jnp.float32
        )
        update = update[: DH + 8]
        if not chunk.diagonal:
            update = acc[u] * jnp.concatenate([factor] * (DH // 8 + 1), axis=0) + update
        acc[u] = update
        return update

    def finish_unit(u, i, value):
        g = pair_of(u, i)
        share = 1.0 / value[DH : DH + 8]
        value = (value[:DH] * jnp.concatenate([share] * (DH // 8), axis=0)).T
        for h in range(PAIR):
            att[
                pl.ds(i * SPAN, SPAN), pl.ds(pl.multiple_of((g * PAIR + h) * DH, DH), DH)
            ] = value[h * SPAN : (h + 1) * SPAN].astype(jnp.bfloat16)

    ss, ww = (s0, s1), (p0, p1)

    def steps_of(chunk):
        most = max(1, 8 * 512 // (spans * chunk.size))
        return max(k for k in range(1, most + 1) if pairs % k == 0) * spans

    def attend(group, between, final):
        per = steps_of(group[0])
        turns = units // per

        def turn(j, carry, c, head, tail):
            chunk = group[c]
            (high, factor), late = carry
            for x in range(per):
                u = per * j + x
                now = x % 2
                weigh(chunk, x % spans, high, ss[now], ww[now])
                if x < per - 1 or not tail:
                    after = score(chunk, u + 1, (x + 1) % spans, ss[1 - now])
                elif c + 1 < len(group):
                    after = score(group[c + 1], 0, 0, ss[1 - now])
                else:
                    after = (high, factor)
                if x or not head:
                    value = gather(chunk, u - 1, late, ww[1 - now])
                    if x and final and c == len(group) - 1:
                        finish_unit(u - 1, (x - 1) % spans, value)
                elif c:
                    gather(group[c - 1], units - 1, late, ww[1 - now])
                late = factor
                high, factor = after
            return (high, factor), late

        group[0].stage()
        start = score(group[0], 0, 0, s0)
        carry = start, start[1]
        for c in range(len(group)):
            if turns > 1:
                carry = turn(0, carry, c, True, False)
                if turns > 2:
                    carry = lax.fori_loop(
                        1,
                        turns - 1,
                        lambda j, carry, c=c: turn(j, carry, c, False, False),
                        carry,
                    )
            if c + 1 < len(group):
                between(c + 1)
                group[c + 1].stage()
            carry = turn(turns - 1, carry, c, turns == 1, True)
        value = gather(group[-1], units - 1, carry[1], ww[(per - 1) % 2])
        if final:
            finish_unit(units - 1, spans - 1, value)

            for j in range(turns - 1):
                u = per * j + per - 1
                finish_unit(u, spans - 1, acc[u])

    attend([Chunk([lambda j, t: own[j, t]], SPAN, 0, vts[0], True)], None, False)

    pl.semaphore_wait(barrier, chips + n_page - 1)

    def remote(p, src, owner, index, target):
        return pltpu.make_async_remote_copy(
            src_ref=src,
            dst_ref=bufs[p].at[owner],
            send_sem=send.at[p, index],
            recv_sem=recv.at[p, index],
            device_id={"ctx": target},
            device_id_type=MESH,
        )

    started = []
    for p in range(count):
        part = own.at[:, :, pl.ds(starts[p], PIECES[p])]
        for d in range(1, chips):
            copy = remote(p, part, me, d, ahead(d))
            copy.start()
            started.append(copy)
        copy = remote(p, part, me, 0, sibling)
        copy.start()
        started.append(copy)

    wanted = []
    for s in range(spans):
        device, place = jnp.int32(0), jnp.int32(0)
        for g in range(n * spans):
            hit = slots_ref[g] == me * spans + s
            device = jnp.where(hit, g // spans, device)
            place = jnp.where(hit, g % spans, place)
        wanted.append((device, place))

    def collect(p):
        buf = bufs[p]
        for d in range(1, chips):
            origin = behind(d, core)
            remote(p, buf.at[origin], origin, d, sibling).wait_recv()
            copy = remote(p, buf.at[origin], origin, chips - 1 + d, sibling)
            copy.start()
            started.append(copy)
        for d in range(1, chips):
            origin = behind(d, 1 - core)
            remote(p, buf.at[origin], origin, chips - 1 + d, sibling).wait_recv()
        select(p)
        publish(p)

    def page_copy(p, index, target, origin):
        ref = zbufs[p].at[origin]
        return pltpu.make_async_remote_copy(
            src_ref=ref,
            dst_ref=ref,
            send_sem=page_send.at[p, index],
            recv_sem=page_recv.at[p, index],
            device_id={"page": target},
            device_id_type=MESH,
        )

    def select(p):
        for s in range(spans):
            device, place = wanted[s]
            for j in range(2):
                zbufs[p][page, j, s] = bufs[p][device, j, place]

    def publish(p):
        for index in range(1, n_page):
            copy = page_copy(p, index, (page + index) % n_page, page)
            copy.start()
            started.append(copy)

    for p in range(count):
        mine[p].wait()
        remote(p, bufs[p].at[sibling], sibling, 0, sibling).wait_recv()

    def beside(j, t):
        return jnp.concatenate([bufs[p][sibling, j, t] for p in range(count)], axis=0)

    attend([Chunk([beside], SPAN, 1, vts[0], False)], None, False)

    collect(0)
    group = [
        Chunk(
            [lambda j, t, p=p, device=device: bufs[p][device, j, t] for device in order[2:]],
            PIECES[p], 2, vts[p % 2], False,
        )
        for p in range(count)
    ]
    attend(group, collect, True)

    finish = pltpu.make_async_copy(att, att_out, out_sem.at[0])
    finish.start()

    for p in range(count):
        for index in range(1, n_page):
            origin = (page + n_page - index) % n_page
            page_copy(p, index, page, origin).wait_recv()

    lanes = lax.broadcasted_iota(jnp.int32, (8, DH), 1)
    for s in range(spans):
        for j in range(2):
            levels = jnp.zeros((8, DH), jnp.float32)
            for h in range(n_page):
                level = None
                for p in range(count):
                    high = jnp.max(jnp.abs(zbufs[p][h, j, s].astype(jnp.float32)), axis=0, keepdims=True)
                    level = high if level is None else jnp.maximum(level, high)
                level = jnp.max(level, axis=1, keepdims=True) + 1e-06
                share = 1.0 / level
                for p in range(count):
                    cache[s, h, j, starts[p] : starts[p] + PIECES[p]] = (
                        zbufs[p][h, j, s].astype(jnp.float32) * share
                    ).astype(jnp.bfloat16)
                levels = jnp.where(lanes == h, level, levels)
            scales[s, j] = levels
    last = [
        pltpu.make_async_copy(cache, cache_out, out_sem.at[1]),
        pltpu.make_async_copy(scales, scales_out, out_sem.at[2]),
    ]
    for copy in last:
        copy.start()
    for copy in started:
        copy.wait_send()
    finish.wait()
    for copy in last:
        copy.wait()


def place_results(att_in, cache_in, scales_in, att_out, cache_out, scales_out, sems):
    moves = [
        pltpu.make_async_copy(att_in, att_out, sems.at[0]),
        pltpu.make_async_copy(cache_in, cache_out, sems.at[1]),
    ]
    for copy in moves:
        copy.start()
    for s in range(scales_out.shape[0]):
        for j in range(scales_out.shape[1]):
            scales_out[s, j : j + 1] = scales_in[s, j, :1, : scales_out.shape[2]]
    for copy in moves:
        copy.wait()


def on_device(n, n_page, queries, keys, values, span_table, page_slots):
    rows = queries.shape[0]
    heads = queries.shape[1] // DH
    spans = rows // SPAN
    units = heads // PAIR * spans
    wide = PAIR * SPAN
    most = max(spans * SPAN, max((n - 2) * spans * p for p in PIECES))
    padded = -(-most // 128) * 128
    any_space = pl.BlockSpec(memory_space=pl.ANY)
    vmem = pl.BlockSpec(memory_space=pltpu.VMEM)
    hbm = pl.BlockSpec(memory_space=pltpu.HBM)
    count = len(PIECES)
    results = (
        jax.ShapeDtypeStruct((rows, heads * DH), jnp.bfloat16),
        jax.ShapeDtypeStruct((spans, n_page, 2, PAGE, DH), jnp.bfloat16),
        jax.ShapeDtypeStruct((spans, 2, 8, DH), jnp.float32),
    )
    attended, cache, scales = pl.pallas_call(
        functools.partial(kernel, n, n_page, heads, spans),
        out_shape=results,
        in_specs=[hbm] * 5,
        out_specs=(any_space,) * 3,
        scratch_shapes=[
            pltpu.SMEM(span_table.shape, jnp.int32),
            pltpu.SMEM(page_slots.shape, jnp.int32),
            pltpu.SMEM((spans * n * spans,), jnp.float32),
            pltpu.VMEM(queries.shape, jnp.bfloat16),
            pltpu.VMEM((2, spans, SPAN, DH), jnp.bfloat16),
            [pltpu.VMEM((DH + 16, padded), jnp.bfloat16)] * 2,
            pltpu.VMEM((most, wide), jnp.float32),
            pltpu.VMEM((most, wide), jnp.float32),
            pltpu.VMEM((most, wide), jnp.bfloat16),
            pltpu.VMEM((most, wide), jnp.bfloat16),
            pltpu.VMEM((units, 8, wide), jnp.float32),
            pltpu.VMEM((units, DH + 8, wide), jnp.float32),
            pltpu.VMEM(queries.shape, jnp.bfloat16),
            pltpu.VMEM((spans, n_page, 2, PAGE, DH), jnp.bfloat16),
            pltpu.VMEM((spans, 2, 8, DH), jnp.float32),
            pltpu.SemaphoreType.DMA((count, n)),
            pltpu.SemaphoreType.DMA((count, n)),
            pltpu.SemaphoreType.DMA((5 + count,)),
            pltpu.SemaphoreType.DMA((count, n_page)),
            pltpu.SemaphoreType.DMA((count, n_page)),
            pltpu.SemaphoreType.DMA((3,)),
        ]
        + [pltpu.VMEM((n, 2, spans, p, DH), jnp.bfloat16) for p in PIECES]
        + [pltpu.VMEM((n_page, 2, spans, p, DH), jnp.bfloat16) for p in PIECES],
        compiler_params=pltpu.CompilerParams(
            collective_id=0, has_side_effects=True, vmem_limit_bytes=48 * 2**20
        ),
    )(
        *(
            pltpu.with_memory_space_constraint(x, pltpu.HBM)
            for x in (
                span_table,
                page_slots,
                queries,
                keys.reshape(spans, SPAN, DH),
                values.reshape(spans, SPAN, DH),
            )
        )
    )
    attended, cache, scales = pl.pallas_call(
        place_results,
        out_shape=results[:2] + (jax.ShapeDtypeStruct((spans, 2, n_page), jnp.float32),),
        in_specs=[any_space, any_space, vmem],
        out_specs=(any_space, any_space, vmem),
        scratch_shapes=[
            pltpu.SemaphoreType.DMA((2,)),
        ],
        compiler_params=pltpu.CompilerParams(vmem_limit_bytes=16 * 2**20),
    )(attended, cache, scales)
    return attended, cache, scales.transpose(0, 2, 1)


def solution(mesh):
    placed = (P("ctx", "page"), P("ctx", "page"), P("ctx", "page"), P(), P())
    return jax.shard_map(
        functools.partial(on_device, mesh.shape["ctx"], mesh.shape["page"]),
        mesh=mesh,
        in_specs=placed,
        out_specs=(P("ctx", "page"), P("ctx", None, None, None, None), P("ctx", None, None)),
        check_vma=False,
    )
```

time: 36.2 us -> 28.8 us (0.80)
  Pallas kernels: 31.7 us -> 28.1 us
  local copies, waits for them, and re-layouts: 3.56 us -> 0 us
    unnamed x10 -> x0, local copies, waits for them, and re-layouts: 3.56 us -> none
    pallas_call x1, Pallas kernels: 29.8 us -> 26.3 us  [on_device(): pl.pallas_call(functools.partial(kernel, n, n_page, heads, spans), out_sh...]
where the time goes in v2:
time: 28.8 us; the launch traced here: 28.7 us
  Pallas kernels  28.1 us (98%)
  between operations  0.64 us (2%)
    pallas_call x1, Pallas kernels, on_device(): pl.pallas_call(functools.partial(kernel, n, n_page, heads, spans), out_sh...  26.3 us
    pallas_call x1, Pallas kernels, on_device(): pl.pallas_call(place_results, out_shape=results[:2] + (jax.ShapeDtypeStru...  1.73 us

profile of v2, /device:TPU:0, one launch (start us, length us, event | category | flops | bytes accessed | tf_op | source)
XLA Modules:
  0.0 28.7 jit_solution(15758940697852247300)
XLA Ops:
  0.6 26.3 %shard_map.76 = (bf16[256,2048]{1,0:T(8,128)(2,1)S(1)}, bf16[2,4,2,128,128]{4,3,2,1,0:T(8,128)(2,1)S(1)}, f32[2,2,8,128]{3,2,1,0:T(8,128)S(1)}) custom-call(s32[16]{0:T(128)} %table_in.1, s32[16]{0:T(128)} %slots_in.1, bf16[256,2048]{1,0:T(8,128)(2,1)} %q_in.1, bf16[2,128,128]{2,1,0:T(8,128)(2,1)} %bitcast.3, bf16[2,128,128]{2,1,0:T(8,128)(2,1)} %bitcast.4), custom_call_target="tpu_custom_call" | custom-call | tf_op jit(solution)/shard_map/pallas_call | solution.py:404
  27.0 1.7 %shard_map.77 = (bf16[256,2048]{1,0:T(8,128)(2,1)}, bf16[2,4,2,128,128]{4,3,2,1,0:T(8,128)(2,1)}, f32[2,2,4]{2,1,0:T(2,128)}) custom-call(bf16[256,2048]{1,0:T(8,128)(2,1)S(1)} %get-tuple-element.9.att_in, bf16[2,4,2,128,128]{4,3,2,1,0:T(8,128)(2,1)S(1)} %get-tuple-element.10.cache_in, f32[2,2,8,128]{3,2,1,0:T(8,128)S(1)} %get-tuple-element.11.scales_in), custom_call_target="tpu_custom_call" | custom-call | tf_op jit(solution)/shard_map/pallas_call | solution.py:449

commit v3 on v2

--- a/solution.py
+++ b/solution.py
@@ -21,7 +21,7 @@
     n, n_page, heads, spans, table_in, slots_in, q_in, k_in, v_in,
     att_out, cache_out, scales_out,
     table_ref, slots_ref, bias, q_ref, own, vts, s0, s1, p0, p1,
-    tops, acc, att, cache, scales, send, recv, own_sem, page_send, page_recv, out_sem,
+    tops, acc, att, cache, scales, send, recv, own_sem, page_send, page_recv, far_send, far_recv, out_sem, fbuf,
     *pieces,
 ):
     count = len(PIECES)
@@ -60,23 +60,67 @@
         copy.start()
         local.append(copy)
 
-    fetch(q_in, q_ref, 0)
-    fetch(k_in, own.at[0], 1)
-    fetch(v_in, own.at[1], 2)
-    fetch(table_in, table_ref, 3)
+    fetch(k_in, own.at[0], 0)
+    fetch(v_in, own.at[1], 1)
+    fetch(table_in, table_ref, 2)
+    fetch(q_in, q_ref, 3)
     fetch(slots_in, slots_ref, 4)
+
+    pl.semaphore_wait(barrier, chips + n_page - 1)
+
+    def remote(p, src, owner, index, target):
+        return pltpu.make_async_remote_copy(
+            src_ref=src,
+            dst_ref=bufs[p].at[owner],
+            send_sem=send.at[p, index],
+            recv_sem=recv.at[p, index],
+            device_id={"ctx": target},
+            device_id_type=MESH,
+        )
+
+    started = []
+
+    def launch(copy):
+        copy.start()
+        started.append(copy)
+
+    def await_piece(p, owner, index):
+        remote(p, bufs[p].at[owner], owner, index, sibling).wait_recv()
+
+    def piece_of(p):
+        return own.at[:, :, pl.ds(starts[p], PIECES[p])]
+
+    def spread(p):
+        for d in range(1, chips):
+            launch(remote(p, piece_of(p), me, d, ahead(d)))
+
+    def across(index):
+        return pltpu.make_async_remote_copy(
+            src_ref=piece_of(count - 1),
+            dst_ref=fbuf.at[me, n_page - index - 1],
+            send_sem=page_send.at[count - 1, index],
+            recv_sem=page_recv.at[count - 1, index],
+            device_id={"page": (page + index) % n_page},
+            device_id_type=MESH,
+        )
+
+    for copy in local[:2]:
+        copy.wait()
+    spread(0)
+    for index in range(1, n_page):
+        launch(across(index))
+    for p in range(count):
+        launch(remote(p, piece_of(p), me, 0, sibling))
 
     rows_at = lax.broadcasted_iota(jnp.int32, (SPAN, wide), 1) % SPAN
     keys_at = lax.broadcasted_iota(jnp.int32, (SPAN, wide), 0)
     for vt in vts:
         vt[DH:, :] = jnp.ones((vt.shape[0] - DH, vt.shape[1]), jnp.bfloat16)
-    for copy in local:
+    for copy in local[2:]:
         copy.wait()
     mine = []
     for p in range(count):
-        copy = pltpu.make_async_copy(
-            own.at[:, :, pl.ds(starts[p], PIECES[p])], bufs[p].at[me], own_sem.at[5 + p]
-        )
+        copy = pltpu.make_async_copy(piece_of(p), bufs[p].at[me], own_sem.at[5 + p])
         copy.start()
         mine.append(copy)
 
@@ -187,10 +231,10 @@
     ss, ww = (s0, s1), (p0, p1)
 
     def steps_of(chunk):
-        most = max(1, 8 * 512 // (spans * chunk.size))
+        most = min(pairs // 2, max(1, 8 * 512 // (spans * chunk.size)))
         return max(k for k in range(1, most + 1) if pairs % k == 0) * spans
 
-    def attend(group, between, final):
+    def attend(group, early, between, final):
         per = steps_of(group[0])
         turns = units // per
 
@@ -221,6 +265,7 @@
         start = score(group[0], 0, 0, s0)
         carry = start, start[1]
         for c in range(len(group)):
+            early(c)
             if turns > 1:
                 carry = turn(0, carry, c, True, False)
                 if turns > 2:
@@ -230,8 +275,8 @@
                         lambda j, carry, c=c: turn(j, carry, c, False, False),
                         carry,
                     )
+            between(c)
             if c + 1 < len(group):
-                between(c + 1)
                 group[c + 1].stage()
             carry = turn(turns - 1, carry, c, turns == 1, True)
         value = gather(group[-1], units - 1, carry[1], ww[(per - 1) % 2])
@@ -242,30 +287,19 @@
                 u = per * j + per - 1
                 finish_unit(u, spans - 1, acc[u])
 
-    attend([Chunk([lambda j, t: own[j, t]], SPAN, 0, vts[0], True)], None, False)
-
-    pl.semaphore_wait(barrier, chips + n_page - 1)
-
-    def remote(p, src, owner, index, target):
-        return pltpu.make_async_remote_copy(
-            src_ref=src,
-            dst_ref=bufs[p].at[owner],
-            send_sem=send.at[p, index],
-            recv_sem=recv.at[p, index],
-            device_id={"ctx": target},
-            device_id_type=MESH,
-        )
-
-    started = []
-    for p in range(count):
-        part = own.at[:, :, pl.ds(starts[p], PIECES[p])]
-        for d in range(1, chips):
-            copy = remote(p, part, me, d, ahead(d))
-            copy.start()
-            started.append(copy)
-        copy = remote(p, part, me, 0, sibling)
-        copy.start()
-        started.append(copy)
+    def idle(c):
+        pass
+
+    def spread_some(k):
+        for p in range(1, count):
+            if min(p, 3) == k:
+                spread(p)
+
+    attend(
+        [Chunk([lambda j, t: own[j, t]], SPAN, 0, vts[0], True)],
+        idle, lambda c: spread_some(1), False,
+    )
+    spread_some(2)
 
     wanted = []
     for s in range(spans):
@@ -276,19 +310,18 @@
             place = jnp.where(hit, g % spans, place)
         wanted.append((device, place))
 
-    def collect(p):
-        buf = bufs[p]
+    def relay(p):
         for d in range(1, chips):
             origin = behind(d, core)
-            remote(p, buf.at[origin], origin, d, sibling).wait_recv()
-            copy = remote(p, buf.at[origin], origin, chips - 1 + d, sibling)
-            copy.start()
-            started.append(copy)
+            await_piece(p, origin, d)
+            launch(remote(p, bufs[p].at[origin], origin, chips - 1 + d, sibling))
+
+    def complete(p):
         for d in range(1, chips):
-            origin = behind(d, 1 - core)
-            remote(p, buf.at[origin], origin, chips - 1 + d, sibling).wait_recv()
+            await_piece(p, behind(d, 1 - core), chips - 1 + d)
         select(p)
-        publish(p)
+        if p < count - 1:
+            publish(p)
 
     def page_copy(p, index, target, origin):
         ref = zbufs[p].at[origin]
@@ -309,20 +342,56 @@
 
     def publish(p):
         for index in range(1, n_page):
-            copy = page_copy(p, index, (page + index) % n_page, page)
-            copy.start()
-            started.append(copy)
+            launch(page_copy(p, index, (page + index) % n_page, page))
+
+    def foreign(index, owner, target):
+        ref = fbuf.at[owner]
+        return pltpu.make_async_remote_copy(
+            src_ref=ref,
+            dst_ref=ref,
+            send_sem=far_send.at[index],
+            recv_sem=far_recv.at[index],
+            device_id={"ctx": target},
+            device_id_type=MESH,
+        )
+
+    def foreign_spread():
+        for index in range(1, n_page):
+            across(index).wait_recv()
+        for d in range(1, chips):
+            launch(foreign(d, me, ahead(d)))
+        launch(foreign(0, me, sibling))
+
+    def foreign_relay():
+        for d in range(1, chips):
+            origin = behind(d, core)
+            foreign(d, origin, sibling).wait_recv()
+            launch(foreign(chips - 1 + d, origin, sibling))
+
+    def foreign_complete():
+        foreign(0, sibling, sibling).wait_recv()
+        for d in range(1, chips):
+            foreign(chips - 1 + d, behind(d, 1 - core), sibling).wait_recv()
+        for s in range(spans):
+            device, place = wanted[s]
+            for k in range(1, n_page):
+                for j in range(2):
+                    zbufs[count - 1][(page + k) % n_page, j, s] = fbuf[device, k - 1, j, place]
 
     for p in range(count):
         mine[p].wait()
-        remote(p, bufs[p].at[sibling], sibling, 0, sibling).wait_recv()
+        await_piece(p, sibling, 0)
 
     def beside(j, t):
         return jnp.concatenate([bufs[p][sibling, j, t] for p in range(count)], axis=0)
 
-    attend([Chunk([beside], SPAN, 1, vts[0], False)], None, False)
-
-    collect(0)
+    def meet(c):
+        spread_some(3)
+        relay(0)
+
+    attend([Chunk([beside], SPAN, 1, vts[0], False)], idle, meet, False)
+
+    complete(0)
     group = [
         Chunk(
             [lambda j, t, p=p, device=device: bufs[p][device, j, t] for device in order[2:]],
@@ -330,15 +399,33 @@
         )
         for p in range(count)
     ]
-    attend(group, collect, True)
+
+    def early(c):
+        if c == 0:
+            relay(1)
+        elif c == 1:
+            complete(2)
+            relay(3)
+        elif c == 3:
+            foreign_relay()
+
+    def between(c):
+        if c == 0:
+            complete(1)
+            foreign_spread()
+            relay(2)
+        elif c == 1:
+            complete(3)
+
+    attend(group, early, between, True)
+    foreign_complete()
 
     finish = pltpu.make_async_copy(att, att_out, out_sem.at[0])
     finish.start()
 
-    for p in range(count):
+    for p in range(count - 1):
         for index in range(1, n_page):
-            origin = (page + n_page - index) % n_page
-            page_copy(p, index, page, origin).wait_recv()
+            page_copy(p, index, page, (page + n_page - index) % n_page).wait_recv()
 
     lanes = lax.broadcasted_iota(jnp.int32, (8, DH), 1)
     for s in range(spans):
@@ -371,10 +458,13 @@
 
 
 def place_results(att_in, cache_in, scales_in, att_out, cache_out, scales_out, sems):
+    parts = sems.shape[0] - cache_in.shape[0]
+    rows = att_in.shape[0] // parts
     moves = [
-        pltpu.make_async_copy(att_in, att_out, sems.at[0]),
-        pltpu.make_async_copy(cache_in, cache_out, sems.at[1]),
+        (att_in.at[pl.ds(j * rows, rows)], att_out.at[pl.ds(j * rows, rows)]) for j in range(parts)
     ]
+    moves += [(cache_in.at[s], cache_out.at[s]) for s in range(cache_in.shape[0])]
+    moves = [pltpu.make_async_copy(*pair, sems.at[j]) for j, pair in enumerate(moves)]
     for copy in moves:
         copy.start()
     for s in range(scales_out.shape[0]):
@@ -422,12 +512,15 @@
             pltpu.VMEM(queries.shape, jnp.bfloat16),
             pltpu.VMEM((spans, n_page, 2, PAGE, DH), jnp.bfloat16),
             pltpu.VMEM((spans, 2, 8, DH), jnp.float32),
-            pltpu.SemaphoreType.DMA((count, n)),
-            pltpu.SemaphoreType.DMA((count, n)),
+            pltpu.SemaphoreType.DMA((count, n - 1)),
+            pltpu.SemaphoreType.DMA((count, n - 1)),
             pltpu.SemaphoreType.DMA((5 + count,)),
             pltpu.SemaphoreType.DMA((count, n_page)),
             pltpu.SemaphoreType.DMA((count, n_page)),
+            pltpu.SemaphoreType.DMA((n - 1,)),
+            pltpu.SemaphoreType.DMA((n - 1,)),
             pltpu.SemaphoreType.DMA((3,)),
+            pltpu.VMEM((n, n_page - 1, 2, spans, PIECES[-1], DH), jnp.bfloat16),
         ]
         + [pltpu.VMEM((n, 2, spans, p, DH), jnp.bfloat16) for p in PIECES]
         + [pltpu.VMEM((n_page, 2, spans, p, DH), jnp.bfloat16) for p in PIECES],
@@ -452,7 +545,7 @@
         in_specs=[any_space, any_space, vmem],
         out_specs=(any_space, any_space, vmem),
         scratch_shapes=[
-            pltpu.SemaphoreType.DMA((2,)),
+            pltpu.SemaphoreType.DMA((4 + spans,)),
         ],
         compiler_params=pltpu.CompilerParams(vmem_limit_bytes=16 * 2**20),
     )(attended, cache, scales)

time: 28.8 us -> 25.3 us (0.88)
  Pallas kernels: 28.1 us -> 24.5 us
    pallas_call x1, Pallas kernels: 26.3 us -> 22.7 us  [on_device(): pl.pallas_call(functools.partial(kernel, n, n_page, heads, spans), out_sh...]
where the time goes in v3:
time: 25.3 us; the launch traced here: 25.1 us
  Pallas kernels  24.5 us (97%)
  between operations  0.64 us (3%)
    pallas_call x1, Pallas kernels, on_device(): pl.pallas_call(functools.partial(kernel, n, n_page, heads, spans), out_sh...  22.7 us
    pallas_call x1, Pallas kernels, on_device(): pl.pallas_call(place_results, out_shape=results[:2] + (jax.ShapeDtypeStru...  1.77 us

profile of v3, /device:TPU:0, one launch (start us, length us, event | category | flops | bytes accessed | tf_op | source)
XLA Modules:
  0.0 25.1 jit_solution(15855373703559506886)
XLA Ops:
  0.6 22.7 %shard_map.76 = (bf16[256,2048]{1,0:T(8,128)(2,1)S(1)}, bf16[2,4,2,128,128]{4,3,2,1,0:T(8,128)(2,1)S(1)}, f32[2,2,8,128]{3,2,1,0:T(8,128)S(1)}) custom-call(s32[16]{0:T(128)} %table_in.1, s32[16]{0:T(128)} %slots_in.1, bf16[256,2048]{1,0:T(8,128)(2,1)} %q_in.1, bf16[2,128,128]{2,1,0:T(8,128)(2,1)} %bitcast.3, bf16[2,128,128]{2,1,0:T(8,128)(2,1)} %bitcast.4), custom_call_target="tpu_custom_call" | custom-call | tf_op jit(solution)/shard_map/pallas_call | solution.py:494
  23.3 1.8 %shard_map.77 = (bf16[256,2048]{1,0:T(8,128)(2,1)}, bf16[2,4,2,128,128]{4,3,2,1,0:T(8,128)(2,1)}, f32[2,2,4]{2,1,0:T(2,128)}) custom-call(bf16[256,2048]{1,0:T(8,128)(2,1)S(1)} %get-tuple-element.9.att_in, bf16[2,4,2,128,128]{4,3,2,1,0:T(8,128)(2,1)S(1)} %get-tuple-element.10.cache_in, f32[2,2,8,128]{3,2,1,0:T(8,128)S(1)} %get-tuple-element.11.scales_in), custom_call_target="tpu_custom_call" | custom-call | tf_op jit(solution)/shard_map/pallas_call | solution.py:542

commit v4 on v3

--- a/solution.py
+++ b/solution.py
@@ -14,6 +14,7 @@
 HIDE = -1e30
 PAIR = 2
 PIECES = (32, 32, 32, 32)
+CHUNKS = ((0,), (1,), (2, 3))
 MESH = pl.DeviceIdType.MESH
 
 
@@ -72,17 +73,22 @@
         return pltpu.make_async_remote_copy(
             src_ref=src,
             dst_ref=bufs[p].at[owner],
-            send_sem=send.at[p, index],
+            send_sem=send.at[p],
             recv_sem=recv.at[p, index],
             device_id={"ctx": target},
             device_id_type=MESH,
         )
 
-    started = []
-
-    def launch(copy):
-        copy.start()
-        started.append(copy)
+    def several(ref, copies, send_sem, recv_sem):
+        some = ref.at[pl.ds(0, copies)]
+        return pltpu.make_async_remote_copy(
+            src_ref=some,
+            dst_ref=some,
+            send_sem=recv_sem if send_sem is None else send_sem,
+            recv_sem=send_sem if recv_sem is None else recv_sem,
+            device_id={"ctx": sibling},
+            device_id_type=MESH,
+        )
 
     def await_piece(p, owner, index):
         remote(p, bufs[p].at[owner], owner, index, sibling).wait_recv()
@@ -92,14 +98,14 @@
 
     def spread(p):
         for d in range(1, chips):
-            launch(remote(p, piece_of(p), me, d, ahead(d)))
+            remote(p, piece_of(p), me, d, ahead(d)).start()
 
     def across(index):
         return pltpu.make_async_remote_copy(
             src_ref=piece_of(count - 1),
             dst_ref=fbuf.at[me, n_page - index - 1],
-            send_sem=page_send.at[count - 1, index],
-            recv_sem=page_recv.at[count - 1, index],
+            send_sem=page_send.at[count - 1],
+            recv_sem=page_recv.at[count - 1],
             device_id={"page": (page + index) % n_page},
             device_id_type=MESH,
         )
@@ -108,9 +114,9 @@
         copy.wait()
     spread(0)
     for index in range(1, n_page):
-        launch(across(index))
+        across(index).start()
     for p in range(count):
-        launch(remote(p, piece_of(p), me, 0, sibling))
+        remote(p, piece_of(p), me, 0, sibling).start()
 
     rows_at = lax.broadcasted_iota(jnp.int32, (SPAN, wide), 1) % SPAN
     keys_at = lax.broadcasted_iota(jnp.int32, (SPAN, wide), 0)
@@ -163,18 +169,21 @@
 
     def score(chunk, u, i, s):
         g = pair_of(u, i)
-        query = jnp.concatenate(
+        keys = chunk.keys()
+        value = jnp.concatenate(
             [
-                q_ref[
-                    pl.ds(i * SPAN, SPAN),
-                    pl.ds(pl.multiple_of((g * PAIR + h) * DH, DH), DH),
-                ]
+                lax.dot_general(
+                    keys,
+                    q_ref[
+                        pl.ds(i * SPAN, SPAN),
+                        pl.ds(pl.multiple_of((g * PAIR + h) * DH, DH), DH),
+                    ],
+                    (((1,), (1,)), ((), ())),
+                    preferred_element_type=jnp.float32,
+                )
                 for h in range(PAIR)
             ],
-            axis=0,
-        )
-        value = lax.dot_general(
-            chunk.keys(), query, (((1,), (1,)), ((), ())), preferred_element_type=jnp.float32
+            axis=1,
         )
         best = None
         rows = chunk.rows
@@ -314,22 +323,21 @@
         for d in range(1, chips):
             origin = behind(d, core)
             await_piece(p, origin, d)
-            launch(remote(p, bufs[p].at[origin], origin, chips - 1 + d, sibling))
+            remote(p, bufs[p].at[origin], origin, chips, sibling).start()
 
     def complete(p):
-        for d in range(1, chips):
-            await_piece(p, behind(d, 1 - core), chips - 1 + d)
+        several(bufs[p], chips - 1, None, recv.at[p, chips]).wait_recv()
         select(p)
         if p < count - 1:
             publish(p)
 
-    def page_copy(p, index, target, origin):
+    def page_copy(p, target, origin):
         ref = zbufs[p].at[origin]
         return pltpu.make_async_remote_copy(
             src_ref=ref,
             dst_ref=ref,
-            send_sem=page_send.at[p, index],
-            recv_sem=page_recv.at[p, index],
+            send_sem=page_send.at[p],
+            recv_sem=page_recv.at[p],
             device_id={"page": target},
             device_id_type=MESH,
         )
@@ -342,36 +350,34 @@
 
     def publish(p):
         for index in range(1, n_page):
-            launch(page_copy(p, index, (page + index) % n_page, page))
+            page_copy(p, (page + index) % n_page, page).start()
 
     def foreign(index, owner, target):
         ref = fbuf.at[owner]
         return pltpu.make_async_remote_copy(
             src_ref=ref,
             dst_ref=ref,
-            send_sem=far_send.at[index],
+            send_sem=far_send.at[0],
             recv_sem=far_recv.at[index],
             device_id={"ctx": target},
             device_id_type=MESH,
         )
 
     def foreign_spread():
-        for index in range(1, n_page):
-            across(index).wait_recv()
+        several(zbufs[count - 1], n_page - 1, None, page_recv.at[count - 1]).wait_recv()
         for d in range(1, chips):
-            launch(foreign(d, me, ahead(d)))
-        launch(foreign(0, me, sibling))
+            foreign(d, me, ahead(d)).start()
+        foreign(0, me, sibling).start()
 
     def foreign_relay():
         for d in range(1, chips):
             origin = behind(d, core)
             foreign(d, origin, sibling).wait_recv()
-            launch(foreign(chips - 1 + d, origin, sibling))
+            foreign(chips, origin, sibling).start()
 
     def foreign_complete():
         foreign(0, sibling, sibling).wait_recv()
-        for d in range(1, chips):
-            foreign(chips - 1 + d, behind(d, 1 - core), sibling).wait_recv()
+        several(fbuf, chips - 1, None, far_recv.at[chips]).wait_recv()
         for s in range(spans):
             device, place = wanted[s]
             for k in range(1, n_page):
@@ -392,12 +398,15 @@
     attend([Chunk([beside], SPAN, 1, vts[0], False)], idle, meet, False)
 
     complete(0)
+    def rows_of(some, device):
+        return lambda j, t: jnp.concatenate([bufs[p][device, j, t] for p in some], axis=0)
+
     group = [
         Chunk(
-            [lambda j, t, p=p, device=device: bufs[p][device, j, t] for device in order[2:]],
-            PIECES[p], 2, vts[p % 2], False,
-        )
-        for p in range(count)
+            [rows_of(some, device) for device in order[2:]],
+            sum(PIECES[p] for p in some), 2, vts[c % 2], False,
+        )
+        for c, some in enumerate(CHUNKS)
     ]
 
     def early(c):
@@ -406,8 +415,6 @@
         elif c == 1:
             complete(2)
             relay(3)
-        elif c == 3:
-            foreign_relay()
 
     def between(c):
         if c == 0:
@@ -416,6 +423,8 @@
             relay(2)
         elif c == 1:
             complete(3)
+        else:
+            foreign_relay()
 
     attend(group, early, between, True)
     foreign_complete()
@@ -424,8 +433,7 @@
     finish.start()
 
     for p in range(count - 1):
-        for index in range(1, n_page):
-            page_copy(p, index, page, (page + n_page - index) % n_page).wait_recv()
+        several(zbufs[p], n_page - 1, None, page_recv.at[p]).wait_recv()
 
     lanes = lax.broadcasted_iota(jnp.int32, (8, DH), 1)
     for s in range(spans):
@@ -450,8 +458,10 @@
     ]
     for copy in last:
         copy.start()
-    for copy in started:
-        copy.wait_send()
+    for p in range(count):
+        several(bufs[p], n - 1, send.at[p], None).wait_send()
+        several(zbufs[p], n_page - 1, page_send.at[p], None).wait_send()
+    several(fbuf, n - 1, far_send.at[0], None).wait_send()
     finish.wait()
     for copy in last:
         copy.wait()
@@ -480,7 +490,8 @@
     spans = rows // SPAN
     units = heads // PAIR * spans
     wide = PAIR * SPAN
-    most = max(spans * SPAN, max((n - 2) * spans * p for p in PIECES))
+    rows_most = max(sum(PIECES[p] for p in some) for some in CHUNKS)
+    most = max(spans * SPAN, (n - 2) * spans * rows_most)
     padded = -(-most // 128) * 128
     any_space = pl.BlockSpec(memory_space=pl.ANY)
     vmem = pl.BlockSpec(memory_space=pltpu.VMEM)
@@ -512,13 +523,13 @@
             pltpu.VMEM(queries.shape, jnp.bfloat16),
             pltpu.VMEM((spans, n_page, 2, PAGE, DH), jnp.bfloat16),
             pltpu.VMEM((spans, 2, 8, DH), jnp.float32),
-            pltpu.SemaphoreType.DMA((count, n - 1)),
-            pltpu.SemaphoreType.DMA((count, n - 1)),
+            pltpu.SemaphoreType.DMA((count,)),
+            pltpu.SemaphoreType.DMA((count, n // 2 + 1)),
             pltpu.SemaphoreType.DMA((5 + count,)),
-            pltpu.SemaphoreType.DMA((count, n_page)),
-            pltpu.SemaphoreType.DMA((count, n_page)),
-            pltpu.SemaphoreType.DMA((n - 1,)),
-            pltpu.SemaphoreType.DMA((n - 1,)),
+            pltpu.SemaphoreType.DMA((count,)),
+            pltpu.SemaphoreType.DMA((count,)),
+            pltpu.SemaphoreType.DMA((1,)),
+            pltpu.SemaphoreType.DMA((n // 2 + 1,)),
             pltpu.SemaphoreType.DMA((3,)),
             pltpu.VMEM((n, n_page - 1, 2, spans, PIECES[-1], DH), jnp.bfloat16),
         ]

time: 25.3 us -> 24 us (0.949)
  Pallas kernels: 24.5 us -> 23.2 us
    pallas_call x1, Pallas kernels: 22.7 us -> 21.4 us  [on_device(): pl.pallas_call(functools.partial(kernel, n, n_page, heads, spans), out_sh...]
where the time goes in v4:
time: 24 us; the launch traced here: 23.9 us
  Pallas kernels  23.2 us (97%)
  between operations  0.64 us (3%)
    pallas_call x1, Pallas kernels, on_device(): pl.pallas_call(functools.partial(kernel, n, n_page, heads, spans), out_sh...  21.4 us
    pallas_call x1, Pallas kernels, on_device(): pl.pallas_call(place_results, out_shape=results[:2] + (jax.ShapeDtypeStru...  1.77 us

profile of v4, /device:TPU:0, one launch (start us, length us, event | category | flops | bytes accessed | tf_op | source)
XLA Modules:
  0.0 23.9 jit_solution(18349412990322476265)
XLA Ops:
  0.6 21.4 %shard_map.76 = (bf16[256,2048]{1,0:T(8,128)(2,1)S(1)}, bf16[2,4,2,128,128]{4,3,2,1,0:T(8,128)(2,1)S(1)}, f32[2,2,8,128]{3,2,1,0:T(8,128)S(1)}) custom-call(s32[16]{0:T(128)} %table_in.1, s32[16]{0:T(128)} %slots_in.1, bf16[256,2048]{1,0:T(8,128)(2,1)} %q_in.1, bf16[2,128,128]{2,1,0:T(8,128)(2,1)} %bitcast.3, bf16[2,128,128]{2,1,0:T(8,128)(2,1)} %bitcast.4), custom_call_target="tpu_custom_call" | custom-call | tf_op jit(solution)/shard_map/pallas_call | solution.py:505
  22.1 1.8 %shard_map.77 = (bf16[256,2048]{1,0:T(8,128)(2,1)}, bf16[2,4,2,128,128]{4,3,2,1,0:T(8,128)(2,1)}, f32[2,2,4]{2,1,0:T(2,128)}) custom-call(bf16[256,2048]{1,0:T(8,128)(2,1)S(1)} %get-tuple-element.9.att_in, bf16[2,4,2,128,128]{4,3,2,1,0:T(8,128)(2,1)S(1)} %get-tuple-element.10.cache_in, f32[2,2,8,128]{3,2,1,0:T(8,128)S(1)} %get-tuple-element.11.scales_in), custom_call_target="tpu_custom_call" | custom-call | tf_op jit(solution)/shard_map/pallas_call | solution.py:553

commit v5 on v4

--- a/solution.py
+++ b/solution.py
@@ -15,6 +15,7 @@
 PAIR = 2
 PIECES = (32, 32, 32, 32)
 CHUNKS = ((0,), (1,), (2, 3))
+HANDED = (0,)
 MESH = pl.DeviceIdType.MESH
 
 
@@ -331,16 +332,24 @@
         if p < count - 1:
             publish(p)
 
-    def page_copy(p, target, origin):
+    def page_copy(p, target, origin, held=False):
         ref = zbufs[p].at[origin]
         return pltpu.make_async_remote_copy(
             src_ref=ref,
             dst_ref=ref,
             send_sem=page_send.at[p],
-            recv_sem=page_recv.at[p],
+            recv_sem=page_recv.at[count + p if held else p],
             device_id={"page": target},
             device_id_type=MESH,
         )
+
+    def within(place):
+        return jnp.logical_and(place >= 0, place < n_page)
+
+    def handed(p):
+        return n_page == 4 and p in HANDED
+
+    inner = jnp.logical_and(page > 0, page < n_page - 1)
 
     def select(p):
         for s in range(spans):
@@ -349,8 +358,43 @@
                 zbufs[p][page, j, s] = bufs[p][device, j, place]
 
     def publish(p):
-        for index in range(1, n_page):
-            page_copy(p, (page + index) % n_page, page).start()
+        if not handed(p):
+            for index in range(1, n_page):
+                page_copy(p, (page + index) % n_page, page).start()
+            return
+        for sign in (-1, 1):
+            @pl.when(within(page + sign))
+            def _(sign=sign):
+                page_copy(p, page + sign, page).start()
+
+            @pl.when(within(page + 3 * sign))
+            def _(sign=sign):
+                page_copy(p, page + 2 * sign, page, True).start()
+
+            @pl.when(jnp.logical_and(within(page + 2 * sign), inner))
+            def _(sign=sign):
+                page_copy(p, page + 2 * sign, page).start()
+
+    def hand_on(p):
+        if handed(p):
+            for sign in (-1, 1):
+                @pl.when(jnp.logical_and(within(page - 2 * sign), inner))
+                def _(sign=sign):
+                    page_copy(p, page + sign, page - 2 * sign, True).wait_recv()
+                    page_copy(p, page + sign, page - 2 * sign).start()
+
+    def each_amount(p, outer_count, inner_count, action):
+        if not handed(p):
+            action(n_page - 1)
+            return
+
+        @pl.when(inner)
+        def _():
+            action(inner_count)
+
+        @pl.when(jnp.logical_not(inner))
+        def _():
+            action(outer_count)
 
     def foreign(index, owner, target):
         ref = fbuf.at[owner]
@@ -411,6 +455,7 @@
 
     def early(c):
         if c == 0:
+            foreign_spread()
             relay(1)
         elif c == 1:
             complete(2)
@@ -419,12 +464,13 @@
     def between(c):
         if c == 0:
             complete(1)
-            foreign_spread()
             relay(2)
         elif c == 1:
             complete(3)
+            hand_on(0)
         else:
             foreign_relay()
+            hand_on(1)
 
     attend(group, early, between, True)
     foreign_complete()
@@ -433,7 +479,9 @@
     finish.start()
 
     for p in range(count - 1):
-        several(zbufs[p], n_page - 1, None, page_recv.at[p]).wait_recv()
+        each_amount(
+            p, 3, 2, lambda k, p=p: several(zbufs[p], k, None, page_recv.at[p]).wait_recv()
+        )
 
     lanes = lax.broadcasted_iota(jnp.int32, (8, DH), 1)
     for s in range(spans):
@@ -460,7 +508,9 @@
         copy.start()
     for p in range(count):
         several(bufs[p], n - 1, send.at[p], None).wait_send()
-        several(zbufs[p], n_page - 1, page_send.at[p], None).wait_send()
+        each_amount(
+            p, 2, 4, lambda k, p=p: several(zbufs[p], k, page_send.at[p], None).wait_send()
+        )
     several(fbuf, n - 1, far_send.at[0], None).wait_send()
     finish.wait()
     for copy in last:
@@ -527,7 +577,7 @@
             pltpu.SemaphoreType.DMA((count, n // 2 + 1)),
             pltpu.SemaphoreType.DMA((5 + count,)),
             pltpu.SemaphoreType.DMA((count,)),
-            pltpu.SemaphoreType.DMA((count,)),
+            pltpu.SemaphoreType.DMA((count + len(HANDED),)),
             pltpu.SemaphoreType.DMA((1,)),
             pltpu.SemaphoreType.DMA((n // 2 + 1,)),
             pltpu.SemaphoreType.DMA((3,)),

time: 24 us -> 23.2 us (0.967)
  Pallas kernels: 23.2 us -> 22.5 us
    pallas_call x1, Pallas kernels: 21.4 us -> 20.7 us  [on_device(): pl.pallas_call(functools.partial(kernel, n, n_page, heads, spans), out_sh...]
where the time goes in v5:
time: 23.2 us; the launch traced here: 23.1 us
  Pallas kernels  22.5 us (97%)
  between operations  0.64 us (3%)
    pallas_call x1, Pallas kernels, on_device(): pl.pallas_call(functools.partial(kernel, n, n_page, heads, spans), out_sh...  20.7 us
    pallas_call x1, Pallas kernels, on_device(): pl.pallas_call(place_results, out_shape=results[:2] + (jax.ShapeDtypeStru...  1.77 us

profile of v5, /device:TPU:0, one launch (start us, length us, event | category | flops | bytes accessed | tf_op | source)
XLA Modules:
  0.0 23.1 jit_solution(593680318322448398)
XLA Ops:
  0.6 20.7 %shard_map.76 = (bf16[256,2048]{1,0:T(8,128)(2,1)S(1)}, bf16[2,4,2,128,128]{4,3,2,1,0:T(8,128)(2,1)S(1)}, f32[2,2,8,128]{3,2,1,0:T(8,128)S(1)}) custom-call(s32[16]{0:T(128)} %table_in.1, s32[16]{0:T(128)} %slots_in.1, bf16[256,2048]{1,0:T(8,128)(2,1)} %q_in.1, bf16[2,128,128]{2,1,0:T(8,128)(2,1)} %bitcast.3, bf16[2,128,128]{2,1,0:T(8,128)(2,1)} %bitcast.4), custom_call_target="tpu_custom_call" | custom-call | tf_op jit(solution)/shard_map/pallas_call | solution.py:555
  21.3 1.8 %shard_map.77 = (bf16[256,2048]{1,0:T(8,128)(2,1)}, bf16[2,4,2,128,128]{4,3,2,1,0:T(8,128)(2,1)}, f32[2,2,4]{2,1,0:T(2,128)}) custom-call(bf16[256,2048]{1,0:T(8,128)(2,1)S(1)} %get-tuple-element.9.att_in, bf16[2,4,2,128,128]{4,3,2,1,0:T(8,128)(2,1)S(1)} %get-tuple-element.10.cache_in, f32[2,2,8,128]{3,2,1,0:T(8,128)S(1)} %get-tuple-element.11.scales_in), custom_call_target="tpu_custom_call" | custom-call | tf_op jit(solution)/shard_map/pallas_call | solution.py:603

commit v6 on v5

--- a/solution.py
+++ b/solution.py
@@ -15,7 +15,7 @@
 PAIR = 2
 PIECES = (32, 32, 32, 32)
 CHUNKS = ((0,), (1,), (2, 3))
-HANDED = (0,)
+HANDED = (0, 1)
 MESH = pl.DeviceIdType.MESH
 
 
@@ -40,11 +40,23 @@
     sibling = 2 * chip + 1 - core
     rate = DH ** (-0.5) * math.log2(math.e)
 
+    even = chips & (chips - 1) == 0
+
+    def across_from(d, back):
+        if not even:
+            return (chip + chips - d) % chips if back else (chip + d) % chips
+        place, bit = chip, 1
+        while bit < chips:
+            if d & bit:
+                place = place + bit * (1 - 2 * (place // bit % 2))
+            bit *= 2
+        return place
+
     def ahead(d):
-        return 2 * ((chip + d) % chips) + core
+        return 2 * across_from(d, False) + core
 
     def behind(d, c):
-        return 2 * ((chip + chips - d) % chips) + c
+        return 2 * across_from(d, True) + c
 
     barrier = pltpu.get_barrier_semaphore()
     for d in range(1, chips):
@@ -98,7 +110,7 @@
         return own.at[:, :, pl.ds(starts[p], PIECES[p])]
 
     def spread(p):
-        for d in range(1, chips):
+        for d in range(chips - 1, 0, -1):
             remote(p, piece_of(p), me, d, ahead(d)).start()
 
     def across(index):
@@ -244,12 +256,11 @@
         most = min(pairs // 2, max(1, 8 * 512 // (spans * chunk.size)))
         return max(k for k in range(1, most + 1) if pairs % k == 0) * spans
 
-    def attend(group, early, between, final):
-        per = steps_of(group[0])
-        turns = units // per
+    def attend(group, early, middle, between, final):
+        pers = [steps_of(chunk) for chunk in group]
 
         def turn(j, carry, c, head, tail):
-            chunk = group[c]
+            chunk, per = group[c], pers[c]
             (high, factor), late = carry
             for x in range(per):
                 u = per * j + x
@@ -275,25 +286,33 @@
         start = score(group[0], 0, 0, s0)
         carry = start, start[1]
         for c in range(len(group)):
+            turns = units // pers[c]
             early(c)
             if turns > 1:
                 carry = turn(0, carry, c, True, False)
-                if turns > 2:
-                    carry = lax.fori_loop(
-                        1,
-                        turns - 1,
-                        lambda j, carry, c=c: turn(j, carry, c, False, False),
-                        carry,
-                    )
+                half = turns // 2
+                for part, (low, high) in enumerate(((1, half), (half, turns - 1))):
+                    if part:
+                        middle(c)
+                    if low < high:
+                        carry = lax.fori_loop(
+                            low,
+                            high,
+                            lambda j, carry, c=c: turn(j, carry, c, False, False),
+                            carry,
+                        )
+            else:
+                middle(c)
             between(c)
             if c + 1 < len(group):
                 group[c + 1].stage()
             carry = turn(turns - 1, carry, c, turns == 1, True)
+        per = pers[-1]
         value = gather(group[-1], units - 1, carry[1], ww[(per - 1) % 2])
         if final:
             finish_unit(units - 1, spans - 1, value)
 
-            for j in range(turns - 1):
+            for j in range(units // per - 1):
                 u = per * j + per - 1
                 finish_unit(u, spans - 1, acc[u])
 
@@ -307,7 +326,7 @@
 
     attend(
         [Chunk([lambda j, t: own[j, t]], SPAN, 0, vts[0], True)],
-        idle, lambda c: spread_some(1), False,
+        idle, idle, lambda c: spread_some(1), False,
     )
     spread_some(2)
 
@@ -439,7 +458,7 @@
         spread_some(3)
         relay(0)
 
-    attend([Chunk([beside], SPAN, 1, vts[0], False)], idle, meet, False)
+    attend([Chunk([beside], SPAN, 1, vts[0], False)], idle, idle, meet, False)
 
     complete(0)
     def rows_of(some, device):
@@ -470,9 +489,12 @@
             hand_on(0)
         else:
             foreign_relay()
+
+    def middle(c):
+        if c == 2:
             hand_on(1)
 
-    attend(group, early, between, True)
+    attend(group, early, middle, between, True)
     foreign_complete()
 
     finish = pltpu.make_async_copy(att, att_out, out_sem.at[0])

time: 23.2 us -> 23.3 us (level)
  no operation moved by 1% of the time
where the time goes in v6:
time: 23.3 us; the launch traced here: 23.1 us
  Pallas kernels  22.5 us (97%)
  between operations  0.64 us (3%)
    pallas_call x1, Pallas kernels, on_device(): pl.pallas_call(functools.partial(kernel, n, n_page, heads, spans), out_sh...  20.7 us
    pallas_call x1, Pallas kernels, on_device(): pl.pallas_call(place_results, out_shape=results[:2] + (jax.ShapeDtypeStru...  1.77 us

profile of v6, /device:TPU:0, one launch (start us, length us, event | category | flops | bytes accessed | tf_op | source)
XLA Modules:
  0.0 23.1 jit_solution(5380365340350474460)
XLA Ops:
  0.6 20.7 %shard_map.76 = (bf16[256,2048]{1,0:T(8,128)(2,1)S(1)}, bf16[2,4,2,128,128]{4,3,2,1,0:T(8,128)(2,1)S(1)}, f32[2,2,8,128]{3,2,1,0:T(8,128)S(1)}) custom-call(s32[16]{0:T(128)} %table_in.1, s32[16]{0:T(128)} %slots_in.1, bf16[256,2048]{1,0:T(8,128)(2,1)} %q_in.1, bf16[2,128,128]{2,1,0:T(8,128)(2,1)} %bitcast.3, bf16[2,128,128]{2,1,0:T(8,128)(2,1)} %bitcast.4), custom_call_target="tpu_custom_call" | custom-call | tf_op jit(solution)/shard_map/pallas_call | solution.py:577
  21.3 1.8 %shard_map.77 = (bf16[256,2048]{1,0:T(8,128)(2,1)}, bf16[2,4,2,128,128]{4,3,2,1,0:T(8,128)(2,1)}, f32[2,2,4]{2,1,0:T(2,128)}) custom-call(bf16[256,2048]{1,0:T(8,128)(2,1)S(1)} %get-tuple-element.9.att_in, bf16[2,4,2,128,128]{4,3,2,1,0:T(8,128)(2,1)S(1)} %get-tuple-element.10.cache_in, f32[2,2,8,128]{3,2,1,0:T(8,128)S(1)} %get-tuple-element.11.scales_in), custom_call_target="tpu_custom_call" | custom-call | tf_op jit(solution)/shard_map/pallas_call | solution.py:625

commit v7 on v6

--- a/solution.py
+++ b/solution.py
@@ -23,7 +23,7 @@
     n, n_page, heads, spans, table_in, slots_in, q_in, k_in, v_in,
     att_out, cache_out, scales_out,
     table_ref, slots_ref, bias, q_ref, own, vts, s0, s1, p0, p1,
-    tops, acc, att, cache, scales, send, recv, own_sem, page_send, page_recv, far_send, far_recv, out_sem, fbuf,
+    tops, acc, att, cache, scales, send, recv, own_sem, page_send, page_recv, far_send, far_recv, fbuf,
     *pieces,
 ):
     count = len(PIECES)
@@ -139,7 +139,7 @@
         copy.wait()
     mine = []
     for p in range(count):
-        copy = pltpu.make_async_copy(piece_of(p), bufs[p].at[me], own_sem.at[5 + p])
+        copy = pltpu.make_async_copy(piece_of(p), bufs[p].at[me], own_sem.at[p])
         copy.start()
         mine.append(copy)
 
@@ -428,7 +428,7 @@
 
     def foreign_spread():
         several(zbufs[count - 1], n_page - 1, None, page_recv.at[count - 1]).wait_recv()
-        for d in range(1, chips):
+        for d in range(chips - 1, 0, -1):
             foreign(d, me, ahead(d)).start()
         foreign(0, me, sibling).start()
 
@@ -497,7 +497,7 @@
     attend(group, early, middle, between, True)
     foreign_complete()
 
-    finish = pltpu.make_async_copy(att, att_out, out_sem.at[0])
+    finish = pltpu.make_async_copy(att, att_out, own_sem.at[0])
     finish.start()
 
     for p in range(count - 1):
@@ -523,8 +523,8 @@
                 levels = jnp.where(lanes == h, level, levels)
             scales[s, j] = levels
     last = [
-        pltpu.make_async_copy(cache, cache_out, out_sem.at[1]),
-        pltpu.make_async_copy(scales, scales_out, out_sem.at[2]),
+        pltpu.make_async_copy(cache, cache_out, own_sem.at[1]),
+        pltpu.make_async_copy(scales, scales_out, own_sem.at[2]),
     ]
     for copy in last:
         copy.start()
@@ -597,12 +597,11 @@
             pltpu.VMEM((spans, 2, 8, DH), jnp.float32),
             pltpu.SemaphoreType.DMA((count,)),
             pltpu.SemaphoreType.DMA((count, n // 2 + 1)),
-            pltpu.SemaphoreType.DMA((5 + count,)),
+            pltpu.SemaphoreType.DMA((max(5, count),)),
             pltpu.SemaphoreType.DMA((count,)),
             pltpu.SemaphoreType.DMA((count + len(HANDED),)),
             pltpu.SemaphoreType.DMA((1,)),
             pltpu.SemaphoreType.DMA((n // 2 + 1,)),
-            pltpu.SemaphoreType.DMA((3,)),
             pltpu.VMEM((n, n_page - 1, 2, spans, PIECES[-1], DH), jnp.bfloat16),
         ]
         + [pltpu.VMEM((n, 2, spans, p, DH), jnp.bfloat16) for p in PIECES]

time: 23.3 us -> 23.2 us (level)
  no operation moved by 1% of the time
where the time goes in v7:
time: 23.2 us; the launch traced here: 23 us
  Pallas kernels  22.4 us (97%)
  between operations  0.64 us (3%)
    pallas_call x1, Pallas kernels, on_device(): pl.pallas_call(functools.partial(kernel, n, n_page, heads, spans), out_sh...  20.6 us
    pallas_call x1, Pallas kernels, on_device(): pl.pallas_call(place_results, out_shape=results[:2] + (jax.ShapeDtypeStru...  1.77 us

profile of v7, /device:TPU:0, one launch (start us, length us, event | category | flops | bytes accessed | tf_op | source)
XLA Modules:
  0.0 23.0 jit_solution(17952913841561293633)
XLA Ops:
  0.6 20.6 %shard_map.76 = (bf16[256,2048]{1,0:T(8,128)(2,1)S(1)}, bf16[2,4,2,128,128]{4,3,2,1,0:T(8,128)(2,1)S(1)}, f32[2,2,8,128]{3,2,1,0:T(8,128)S(1)}) custom-call(s32[16]{0:T(128)} %table_in.1, s32[16]{0:T(128)} %slots_in.1, bf16[256,2048]{1,0:T(8,128)(2,1)} %q_in.1, bf16[2,128,128]{2,1,0:T(8,128)(2,1)} %bitcast.3, bf16[2,128,128]{2,1,0:T(8,128)(2,1)} %bitcast.4), custom_call_target="tpu_custom_call" | custom-call | tf_op jit(solution)/shard_map/pallas_call | solution.py:577
  21.3 1.8 %shard_map.77 = (bf16[256,2048]{1,0:T(8,128)(2,1)}, bf16[2,4,2,128,128]{4,3,2,1,0:T(8,128)(2,1)}, f32[2,2,4]{2,1,0:T(2,128)}) custom-call(bf16[256,2048]{1,0:T(8,128)(2,1)S(1)} %get-tuple-element.9.att_in, bf16[2,4,2,128,128]{4,3,2,1,0:T(8,128)(2,1)S(1)} %get-tuple-element.10.cache_in, f32[2,2,8,128]{3,2,1,0:T(8,128)S(1)} %get-tuple-element.11.scales_in), custom_call_target="tpu_custom_call" | custom-call | tf_op jit(solution)/shard_map/pallas_call | solution.py:624
